TPU v7x, 32 devices: a whole 2x2x4 slice. The times are simulated.
32 devices in a mesh: dp: 8 (over y, x, core), hid: 4 (over z).
Axes of the slice: x: 2, y: 2, z: 4, core: 2. Of those that a mesh axis runs over, the one named last changes fastest.
Arguments:
- tokens: bfloat16 [512, 4096], P(('dp', 'hid')), may hold values from -6 to 6
- cotangent: bfloat16 [512, 7680], P('dp', 'hid'), may hold values from -8 to 8
- weights: bfloat16 [2, 7680, 4096], P(None, 'hid'), may hold values from -0.09375 to 0.09375
- basis: bfloat16 [4096, 256], P('dp'), may hold values from -0.09375 to 0.09375
- master: float32 [2, 7680, 4096], P(None, 'hid', 'dp'), may hold values from -0.09375 to 0.09375
- first_moment: float32 [7680, 2, 256], P(('hid', 'dp')), may hold values from -48 to 48
- second_moment: float32 [7680, 2, 256], P(('hid', 'dp')), may hold values from 25 to 2500
Outputs:
- master_new: float32 [2, 7680, 4096], P(None, 'hid', 'dp')
- first_new: float32 [7680, 2, 256], P(('hid', 'dp'))
- second_new: float32 [7680, 2, 256], P(('hid', 'dp'))
All inputs are finite; a program needn't handle non-finite values.
Results may differ from a plain program's by a relative error of at most 0.0003.
Values may be sent and summed in bfloat16 or wider, within the bound.
No kernel may reach another device: no remote copies, remote signals or barrier semaphores. Data moves between devices by JAX's collectives and lax.ppermute only.
A program may use at most 128 MiB of HBM per device.

v0:
```python
import jax
import jax.numpy as jnp
from jax import lax
from jax.sharding import PartitionSpec as P

beta_first = 0.9
beta_second = 0.95
step_size = 0.05
adam_epsilon = 1e-08


def silu_pieces(pre_gate):
    sigmoid_val = jax.nn.sigmoid(pre_gate)
    return (pre_gate * sigmoid_val, sigmoid_val * (1.0 + pre_gate * (1.0 - sigmoid_val)))


def on_device(tokens, cotangent, weights, basis, master, first_moment, second_moment):
    highest = lax.Precision.HIGHEST
    group_tokens = lax.all_gather(tokens, "hid", axis=0, tiled=True)
    projected = jnp.dot(
        group_tokens,
        lax.all_gather(basis, "dp", axis=0, tiled=True),
        preferred_element_type=jnp.float32,
    )
    contract_cols = (((1,), (1,)), ((), ()))
    pre_gate = lax.dot_general(
        group_tokens, weights[0], contract_cols, preferred_element_type=jnp.float32
    )
    pre_up = lax.dot_general(
        group_tokens, weights[1], contract_cols, preferred_element_type=jnp.float32
    )
    activated, silu_slope = silu_pieces(pre_gate)
    upstream = cotangent.astype(jnp.float32)
    grad_gate = upstream * pre_up * silu_slope
    grad_up = upstream * activated
    over_tokens = (((0,), (0,)), ((), ()))
    gate_term = lax.dot_general(
        grad_gate, projected, over_tokens, precision=highest, preferred_element_type=jnp.float32
    )
    up_term = lax.dot_general(
        grad_up, projected, over_tokens, precision=highest, preferred_element_type=jnp.float32
    )
    gradient = lax.psum_scatter(
        jnp.stack([gate_term, up_term], axis=1), "dp", scatter_dimension=0, tiled=True
    )
    first_new = beta_first * first_moment + (1.0 - beta_first) * gradient
    second_new = beta_second * second_moment + (1.0 - beta_second) * gradient * gradient
    direction_share = first_new / (jnp.sqrt(second_new) + adam_epsilon)
    direction = lax.all_gather(direction_share, "dp", axis=0, tiled=True)
    lifted = jnp.einsum("fwr,dr->wfd", direction, basis.astype(jnp.float32), precision=highest)
    master_new = master - step_size * lifted
    return (master_new, first_new, second_new)


def solution(mesh):
    in_specs = (
        P(("dp", "hid"), None),
        P("dp", "hid"),
        P(None, "hid", None),
        P("dp", None),
        P(None, "hid", "dp"),
        P(("hid", "dp"), None, None),
        P(("hid", "dp"), None, None),
    )
    out_specs = (P(None, "hid", "dp"), P(("hid", "dp"), None, None), P(("hid", "dp"), None, None))
    return jax.shard_map(
        on_device, mesh=mesh, in_specs=in_specs, out_specs=out_specs, check_vma=False
    )
```

profile of v0, /device:TPU:0, one launch (start us, length us, event | category | flops | bytes accessed | tf_op | source)
XLA Modules:
  0.0 156.3 jit_solution(17608231928793287839)
XLA Ops:
  7.2 0.0 all-gather.3.cloned.1.call-start
  7.2 0.7 all-gather.3.cloned.1.call-update
  7.9 0.0 reduce-scatter.2.cloned.1.call-start
  7.9 17.6 %all_gather.9 = bf16[64,4096]{1,0:T(8,128)(2,1)S(1)} all-gather(bf16[16,4096]{1,0:T(8,128)(2,1)} %param.7), channel_id=1, replica_groups=mesh['dp'=8,'hid'=4] {'hid'}, dimensions={0}, use_global_device_ids=true | all-gather | bytes 655360 | tf_op jit(solution)/shard_map/all_gather | solution.py:19
  25.5 8.8 %fusion = f32[64,1920]{1,0:T(8,128)S(1)} fusion(bf16[64,4096]{1,0:T(8,128)(2,1)S(1)} %all_gather.9, bf16[2,1920,4096]{2,1,0:T(8,128)(2,1)} %param.9), kind=kOutput, calls=%fused_computation | convolution fusion | flops 1006632960 | bytes 16744448 | tf_op jit(solution)/shard_map/dot_general | solution.py:26
  34.3 0.0 copy-done.3
  34.3 8.8 %fusion.9 = f32[64,1920]{1,0:T(8,128)S(1)} fusion(bf16[64,4096]{1,0:T(8,128)(2,1)S(1)} %all_gather.9, bf16[2,1920,4096]{2,1,0:T(8,128)(2,1)} %param.9, bf16[64,1920]{1,0:T(8,128)(2,1)S(1)} %copy-done.3, f32[64,1920]{1,0:T(8,128)S(1)} %fusion), kind=kOutput, calls=%fused_computation.11 | convolution fusion | flops 1007861760 | bytes 17481728 | tf_op jit(solution)/shard_map/dot_general | solution.py:29
  43.2 0.0 all-gather.3.cloned.1.call-done
  43.2 2.0 %fusion.20 = f32[64,256]{1,0:T(8,128)S(1)} fusion(bf16[64,4096]{1,0:T(8,128)(2,1)S(1)} %all_gather.9, bf16[4096,256]{1,0:T(8,128)(2,1)} %all-gather.3.cloned.1.call-done), kind=kOutput, calls=%fused_computation.24 | convolution fusion | flops 134217728 | bytes 2686976 | tf_op jit(solution)/shard_map/dot_general | solution.py:20
  45.3 1.8 %convolution_bitcast_fusion = f32[1920,1,256]{2,0,1:T(8,128)S(1)} fusion(f32[64,256]{1,0:T(8,128)S(1)} %fusion.20, bf16[64,1920]{1,0:T(8,128)(2,1)S(1)} %copy-done.3, f32[64,1920]{1,0:T(8,128)S(1)} %fusion), kind=kOutput, calls=%fused_computation.8 | convolution fusion | flops 378224640 | bytes 2768896 | tf_op jit(solution)/shard_map/dot_general | solution.py:40
  47.0 1.8 %convolution_bitcast_fusion.1 = f32[1920,1,256]{2,0,1:T(8,128)S(1)} fusion(f32[64,1920]{1,0:T(8,128)S(1)} %fusion.9, f32[64,256]{1,0:T(8,128)S(1)} %fusion.20), kind=kOutput, calls=%fused_computation.9 | convolution fusion | flops 377487360 | bytes 2523136 | tf_op jit(solution)/shard_map/dot_general | solution.py:37
  48.8 2.2 %pad_maximum_fusion = f32[1920,2,256]{2,0,1:T(8,128)} fusion(f32[1920,1,256]{2,0,1:T(8,128)S(1)} %convolution_bitcast_fusion, f32[1920,1,256]{2,0,1:T(8,128)S(1)} %convolution_bitcast_fusion.1), kind=kLoop, calls=%fused_computation.7 | loop fusion | flops 983040 | bytes 7864320 | tf_op jit(solution)/shard_map/stack | solution.py:44
  51.0 0.0 reduce-scatter.2.cloned.1.call-update
  51.0 0.0 all-gather.5.cloned.1.call-start
  51.1 51.6 %reduce-scatter.2.cloned.1.call-done = f32[240,2,256]{2,0,1:T(8,128)} async-done(((f32[1920,2,256]{2,0,1:T(8,128)}), f32[240,2,256]{2,0,1:T(8,128)}) %reduce-scatter.2.cloned.1.call-update) | async-done | bytes 491536 | tf_op jit(solution)/shard_map/reduce_scatter | solution.py:43
  102.7 0.0 copy-done.1
  102.7 0.0 copy-done.2
  102.7 2.1 %add_divide_fusion = (f32[240,2,256]{2,0,1:T(8,128)}, f32[240,2,256]{2,0,1:T(8,128)S(1)}, f32[240,2,256]{2,0,1:T(8,128)S(1)}) fusion(f32[240,2,256]{2,0,1:T(8,128)} %reduce-scatter.2.cloned.1.call-done, f32[240,2,256]{2,1,0:T(2,128)S(1)} %copy-done.1, f32[240,2,256]{2,1,0:T(2,128)S(1)} %copy-done.2), kind=kLoop, calls=%fused_computation.18 | loop fusion | flops 1105920 | bytes 2949120 | tf_op jit(solution)/shard_map/div | solution.py:48
  104.8 0.0 all-gather.5.cloned.1.call-update
  104.8 1.2 copy.13
  106.0 1.2 copy.12
  107.1 33.5 %all-gather.5.cloned.1.call-done = f32[1920,2,256]{2,0,1:T(8,128)} async-done(((f32[240,2,256]{2,0,1:T(8,128)}), f32[1920,2,256]{2,0,1:T(8,128)}) %all-gather.5.cloned.1.call-update) | async-done | bytes 3932176 | tf_op jit(solution)/shard_map/all_gather | solution.py:49
  140.7 0.0 copy-done
  140.7 9.1 %bitcast_subtract_fusion = f32[2,1920,512]{2,1,0:T(8,128)} fusion(f32[2,1920,512]{2,1,0:T(8,128)} %param.11, f32[1920,2,256]{2,0,1:T(8,128)} %all-gather.5.cloned.1.call-done, bf16[512,256]{1,0:T(8,128)(2,1)S(1)} %copy-done), kind=kOutput, calls=%fused_computation.6 | convolution fusion | flops 6043729920 | bytes 19922944 | tf_op jit(solution)/shard_map/fwr,dr->wfd/dot_general | solution.py:50
  (4 shorter events, 0.0 us)
Async XLA Ops:
  7.2 36.0 %all-gather.3.cloned.1.call-start = ((), (), s32[]{:S(2)}) async-start(), calls=%async_computation.1 | async-start | bytes 2359296 | tf_op jit(solution)/shard_map/all_gather | solution.py:22
  7.9 94.8 %reduce-scatter.2.cloned.1.call-start = ((), (), s32[]{:S(2)}) async-start(), calls=%async_computation.2 | async-start | bytes 4423680 | tf_op jit(solution)/shard_map/reduce_scatter | solution.py:43
  25.5 8.8 %copy-start.3 = (bf16[64,1920]{1,0:T(8,128)(2,1)S(1)}, bf16[64,1920]{1,0:T(8,128)(2,1)}, u32[]{:S(2)}) copy-start(bf16[64,1920]{1,0:T(8,128)(2,1)} %param.8) | copy-start | bytes 737284
  51.0 51.7 %copy-start.1 = (f32[240,2,256]{2,1,0:T(2,128)S(1)}, f32[240,2,256]{2,1,0:T(2,128)}, u32[]{:S(2)}) copy-start(f32[240,2,256]{2,1,0:T(2,128)} %param.13) | copy-start | bytes 1474564
  51.0 51.7 %copy-start.2 = (f32[240,2,256]{2,1,0:T(2,128)S(1)}, f32[240,2,256]{2,1,0:T(2,128)}, u32[]{:S(2)}) copy-start(f32[240,2,256]{2,1,0:T(2,128)} %param.12) | copy-start | bytes 1474564
  51.0 89.7 %copy-start = (bf16[512,256]{1,0:T(8,128)(2,1)S(1)}, bf16[512,256]{1,0:T(8,128)(2,1)}, u32[]{:S(2)}) copy-start(bf16[512,256]{1,0:T(8,128)(2,1)} %param.10) | copy-start | bytes 786436
  51.0 89.7 %all-gather.5.cloned.1.call-start = ((), (), s32[]{:S(2)}) async-start(), calls=%async_computation.3 | async-start | bytes 4423680 | tf_op jit(solution)/shard_map/all_gather | solution.py:49
Sparse Core Ops, SparseCore 0:
  9.9 30.4 all-gather.2
  51.1 51.5 reduce-scatter.1
  105.2 35.4 all-gather.4
where the time goes:
time: 156 us
  waiting for transfers between devices  85.9 us (55%)
  matrix products  32.3 us (21%)
  blocking collectives  17.6 us (11%)
  between operations  13.8 us (9%)
  other arithmetic  4.27 us (3%)
  local copies, waits for them, and re-layouts  2.33 us (1%)
    reduce_scatter x1, waiting for transfers between devices, on_device(): lax.psum_scatter(jnp.stack([gate_term, up_term], axis=1), 'dp', scatter_d...  51.6 us
    all_gather x1, waiting for transfers between devices, on_device(): direction = lax.all_gather(direction_share, 'dp', axis=0, tiled=True)  33.5 us
    all_gather x1, blocking collectives, on_device(): group_tokens = lax.all_gather(tokens, 'hid', axis=0, tiled=True)  17.6 us
    dot_general x1, matrix products, on_device(): jnp.einsum('fwr,dr->wfd', direction, basis.astype(jnp.float32), precision...  9.06 us
    dot_general x1, matrix products, on_device(): lax.dot_general(group_tokens, weights[1], contract_cols, preferred_elemen...  8.84 us
    dot_general x1, matrix products, on_device(): lax.dot_general(group_tokens, weights[0], contract_cols, preferred_elemen...  8.77 us
  transfers between devices with their start and end apart: 3, of which 2 were waited for; matrix products, arithmetic and copies ran while one was open for 13% of the time, Pallas kernels for 0%

commit v1 on v0

--- a/solution.py
+++ b/solution.py
@@ -1,12 +1,27 @@
+import functools
+
 import jax
 import jax.numpy as jnp
 from jax import lax
+from jax.experimental import pallas as pl
+from jax.experimental.pallas import tpu as pltpu
 from jax.sharding import PartitionSpec as P
+
 
 beta_first = 0.9
 beta_second = 0.95
 step_size = 0.05
 adam_epsilon = 1e-08
+code_scale = 4096.0
+code_scale_squarings = 3
+code_top = 240.0
+code_squarings = 4
+tiny = 1e-30
+
+
+VMEM = pl.BlockSpec(memory_space=pltpu.VMEM)
+HBM = pl.BlockSpec(memory_space=pltpu.HBM)
+MIB = 1 << 20
 
 
 def silu_pieces(pre_gate):
@@ -14,7 +29,365 @@
     return (pre_gate * sigmoid_val, sigmoid_val * (1.0 + pre_gate * (1.0 - sigmoid_val)))
 
 
-def on_device(tokens, cotangent, weights, basis, master, first_moment, second_moment):
+def split(x):
+    high = x.astype(jnp.bfloat16)
+    return high, (x - high.astype(jnp.float32)).astype(jnp.bfloat16)
+
+
+def encode(x, scale, squarings):
+    a = jnp.abs(x) * scale
+    for _ in range(squarings):
+        a = a * a
+    return jnp.where(x < 0, -a, a).astype(jnp.bfloat16)
+
+
+def decode(y, inverse_scale, squarings):
+    a = jnp.abs(y)
+    root = jnp.exp(jnp.log(jnp.where(a == 0, 1.0, a)) * 0.5**squarings) * inverse_scale
+    root = jnp.where(a == 0, 0.0, root)
+    return jnp.where(y < 0, -root, root)
+
+
+def scale_for(*terms):
+    most = functools.reduce(jnp.maximum, [jnp.max(jnp.abs(t)) for t in terms])
+    return (code_top / jnp.maximum(jnp.full((1, 1), most), tiny)).astype(jnp.bfloat16)
+
+
+def load_weights_kernel(share, places, w_hbm, out, sem):
+    core = lax.rem(lax.axis_index("dp"), 2)
+    plane = lax.div(lax.axis_index("dp"), 2)
+    copies = []
+    for j in range(places):
+        row = pl.multiple_of((2 * jnp.bitwise_xor(plane, j) + core) * share, 16)
+        copies.append(
+            pltpu.make_async_copy(w_hbm.at[:, pl.ds(row, share)], out.at[j], sem.at[j])
+        )
+    for c in copies:
+        c.start()
+    for c in copies:
+        c.wait()
+
+
+def cotangents_kernel(share, places, cot, own, send):
+    core = lax.rem(lax.axis_index("dp"), 2)
+    for c in range(2):
+
+        @pl.when(core == c)
+        def _():
+            for p in range(places):
+                here, there = 2 * p + c, 2 * p + 1 - c
+                own[p] = cot[:, here * share : (here + 1) * share]
+                send[p] = cot[:, there * share : (there + 1) * share]
+
+
+def project_kernel(places, tok, *refs):
+    bases = refs[:places]
+    out_part, out_send = refs[places:]
+    core = lax.rem(lax.axis_index("dp"), 2)
+    plane = lax.div(lax.axis_index("dp"), 2)
+    depth = bases[0].shape[0]
+    total = None
+    for j in range(places):
+        col = pl.multiple_of((2 * jnp.bitwise_xor(plane, j) + core) * depth, 128)
+        term = jnp.dot(tok[:, pl.ds(col, depth)], bases[j][...], preferred_element_type=jnp.float32)
+        total = term if total is None else total + term
+    half = total.shape[0] // 2
+    out_part[...] = total
+    out_send[:half] = total[half:]
+    out_send[half:] = total[:half]
+
+
+def grads_kernel(j, n_hid, rows, with_tokens, with_projected, extra_projected, *refs):
+    refs = list(refs)
+    pieces = 2 * n_hid if with_tokens else 1
+    toks, (w, cot_own, cot_other) = refs[:pieces], refs[pieces : pieces + 3]
+    refs = refs[pieces + 3 :]
+    part, part_other = (refs.pop(0), refs.pop(0)) if with_projected else (None, None)
+    out = refs[0]
+    tok = toks[0]
+    if with_tokens:
+        tok = refs[1]
+        for i, t in enumerate(toks):
+            tok[i * rows : (i + 1) * rows] = t[...]
+    contract = (((1,), (1,)), ((), ()))
+    plane = lax.div(lax.axis_index("dp"), 2)
+    hid = lax.axis_index("hid")
+    gate = lax.dot_general(tok[...], w[j, 0], contract, preferred_element_type=jnp.float32)
+    up = lax.dot_general(tok[...], w[j, 1], contract, preferred_element_type=jnp.float32)
+    place = jnp.bitwise_xor(plane, j)
+    parts = []
+    for cot in (cot_own, cot_other):
+        for k in range(n_hid):
+            start = pl.multiple_of(jnp.bitwise_xor(hid, k) * rows, rows)
+            parts.append(cot[place, pl.ds(start, rows), :])
+    upstream = jnp.concatenate(parts, axis=0).astype(jnp.float32)
+    activated, slope = silu_pieces(gate)
+    terms = (upstream * up * slope, upstream * activated)
+    n_tok, share = gate.shape
+    if j == 0:
+        out[0], out[1] = terms
+        return
+    scale = scale_for(*terms)
+    wide = scale.astype(jnp.float32)
+    for k in range(2):
+        here = slice(k * n_tok, (k + 1) * n_tok)
+        out[here, :share] = encode(terms[k], wide, code_squarings)
+        out[here, share:] = jnp.broadcast_to(scale, (n_tok, out.shape[1] - share))
+    if with_projected:
+        projected = part[...] + part_other[...]
+        scale = scale_for(projected)
+        coded = encode(projected, scale.astype(jnp.float32), code_squarings)
+        for ref, top in [(out, 2 * n_tok)] + ([(refs[1], 0)] if extra_projected else []):
+            ref[top : top + n_tok] = coded
+            ref[top + n_tok :] = jnp.broadcast_to(scale, (ref.shape[0] - top - n_tok, ref.shape[1]))
+
+
+def adam_kernel(places, share, own_grads, part, part_other, *refs):
+    messages = refs[: places - 1]
+    last_projected, first, second, first_new, second_new, code = refs[places - 1 :]
+    n_tok = part.shape[0]
+    dot = functools.partial(
+        lax.dot_general,
+        dimension_numbers=(((0,), (0,)), ((), ())),
+        preferred_element_type=jnp.float32,
+    )
+    projs = [part[...] + part_other[...]]
+    for i, m in enumerate(messages):
+        ref, top = (m, 2 * n_tok) if i < places - 2 else (last_projected, 0)
+        values = ref[top : top + n_tok].astype(jnp.float32)
+        scale = ref[top + n_tok : top + n_tok + 1, :].astype(jnp.float32)
+        projs.append(decode(values, 1.0 / scale, code_squarings))
+    p_high, p_low = split(jnp.concatenate(projs, axis=0))
+    for k in range(2):
+        parts = [own_grads[k]]
+        for m in messages:
+            values = m[k * n_tok : (k + 1) * n_tok].astype(jnp.float32)
+            scale = values[:, share : share + 1]
+            parts.append(decode(values, 1.0 / scale, code_squarings)[:, :share])
+        g_high, g_low = split(jnp.concatenate(parts, axis=0))
+        gradient = dot(g_high, p_high) + (dot(g_high, p_low) + dot(g_low, p_high))
+        m = beta_first * first[k] + (1.0 - beta_first) * gradient
+        v = beta_second * second[k] + (1.0 - beta_second) * gradient * gradient
+        first_new[k] = m
+        second_new[k] = v
+        code[k] = encode(m / (jnp.sqrt(v) + adam_epsilon), code_scale, code_scale_squarings)
+
+
+def moments_kernel(first, second, first_out, second_out):
+    for k in range(2):
+        first_out[:, k] = first[k]
+        second_out[:, k] = second[k]
+
+
+def load_master_kernel(pieces, hbm, out, sem):
+    rows = out.shape[1] // pieces
+    copies = []
+    for i in range(pieces):
+        at = (slice(None), pl.ds(i * rows, rows))
+        copies.append(pltpu.make_async_copy(hbm.at[at], out.at[at], sem.at[i]))
+    for c in copies:
+        c.start()
+    for c in copies:
+        c.wait()
+
+
+def lift_kernel(share, j, other, *refs):
+    codes, basis, master = refs[:3]
+    out, o_buf, sem = refs[-3:]
+    core = lax.rem(lax.axis_index("dp"), 2)
+    plane = lax.div(lax.axis_index("dp"), 2)
+    who = 2 * jnp.bitwise_xor(plane, j) + jnp.bitwise_xor(core, other)
+    row = pl.ds(pl.multiple_of(who * share, 16), share)
+    copies = []
+    for k in range(2):
+        values = codes[k].astype(jnp.float32)
+        terms = split(decode(values, step_size / code_scale, code_scale_squarings))
+        lifted = jnp.dot(
+            jnp.concatenate(terms, axis=1), basis[...], preferred_element_type=jnp.float32
+        )
+        o_buf[k] = master[k, row, :] - lifted
+        c = pltpu.make_async_copy(o_buf.at[k], out.at[k, row], sem.at[k])
+        c.start()
+        copies.append(c)
+    for c in copies:
+        c.wait()
+
+
+def fast_device(n_dp, n_hid, tokens, cotangent, weights, basis, master, first_moment, second_moment):
+    places = n_dp // 2
+    rows, width = tokens.shape
+    group = rows * n_hid
+    ff = weights.shape[1]
+    share = ff // n_dp
+    depth, rank = basis.shape
+    f32, bf16 = jnp.float32, jnp.bfloat16
+
+    def swap(x, axis, flip):
+        n = n_hid if axis == "hid" else n_dp
+        return lax.ppermute(x, axis, [(i, i ^ flip) for i in range(n)])
+
+    def swap_hid(x, k):
+        return swap(x, "hid", k)
+
+    def swap_plane(x, j):
+        return swap(x, "dp", 2 * j) if j else x
+
+    def swap_core(x):
+        return swap(x, "dp", 1)
+
+    core = lax.rem(lax.axis_index("dp"), 2)
+
+    own = [tokens] + [swap_hid(tokens, k) for k in range(n_hid - 1, 0, -1)][::-1]
+    bases = [basis] + [swap_plane(basis, j) for j in range(1, places)]
+
+    cot_shape = jax.ShapeDtypeStruct((places, group, share), bf16)
+    cot_own, cot_send = pl.pallas_call(
+        functools.partial(cotangents_kernel, share, places),
+        in_specs=[VMEM],
+        out_specs=[VMEM] * 2,
+        out_shape=[cot_shape] * 2,
+        compiler_params=pltpu.CompilerParams(vmem_limit_bytes=4 * MIB),
+        name="cotangents",
+    )(cotangent)
+    cot_other = swap_core(cot_send)
+
+    held = pl.pallas_call(
+        functools.partial(load_weights_kernel, share, places),
+        in_specs=[HBM],
+        out_specs=VMEM,
+        out_shape=pltpu.VMEM((places, 2, share, width), bf16),
+        scratch_shapes=[pltpu.SemaphoreType.DMA((places,))],
+        compiler_params=pltpu.CompilerParams(vmem_limit_bytes=MIB),
+        cost_estimate=pl.CostEstimate(
+            flops=0, bytes_accessed=2 * places * 2 * share * width * 2, transcendentals=0
+        ),
+        name="load_weights",
+    )(pltpu.with_memory_space_constraint(weights, pltpu.HBM))
+
+    other = [swap_core(t) for t in own]
+    messages, part, part_other = {}, None, None
+    n_tok, spare = 2 * group, 16
+    for j in [places - 1, 0] + list(range(places - 2, 0, -1)):
+        first, extra = j == places - 1, j == places - 2
+        with_projected = bool(j) and not first
+        ins = (own + other if first else [toks]) + [held, cot_own, cot_other]
+        ins += [part, part_other] if with_projected else []
+        if not j:
+            shapes = [jax.ShapeDtypeStruct((2, n_tok, share), f32)]
+        else:
+            depth_of = 2 * n_tok + (n_tok + spare if with_projected else 0)
+            shapes = [jax.ShapeDtypeStruct((depth_of, rank), bf16)]
+        if first:
+            shapes.append(jax.ShapeDtypeStruct((n_tok, width), bf16))
+        if extra:
+            shapes.append(jax.ShapeDtypeStruct((n_tok + spare, rank), bf16))
+        outs = pl.pallas_call(
+            functools.partial(grads_kernel, j, n_hid, rows, first, with_projected, extra),
+            in_specs=[VMEM] * len(ins),
+            out_specs=[VMEM] * len(shapes),
+            out_shape=shapes,
+            compiler_params=pltpu.CompilerParams(vmem_limit_bytes=16 * MIB),
+            cost_estimate=pl.CostEstimate(
+                flops=2 * n_tok * 2 * share * width,
+                bytes_accessed=2 * share * width * 2,
+                transcendentals=n_tok * share,
+            ),
+        )(*ins)
+        messages[j] = swap_plane(outs[0], j)
+        if first:
+            toks = outs[1]
+            part_shape = jax.ShapeDtypeStruct((n_tok, rank), f32)
+            part, part_send = pl.pallas_call(
+                functools.partial(project_kernel, places),
+                in_specs=[VMEM] * (1 + places),
+                out_specs=[VMEM] * 2,
+                out_shape=[part_shape] * 2,
+                compiler_params=pltpu.CompilerParams(vmem_limit_bytes=16 * MIB),
+                cost_estimate=pl.CostEstimate(
+                    flops=2 * n_tok * places * depth * rank,
+                    bytes_accessed=n_tok * width * 2,
+                    transcendentals=0,
+                ),
+                name="project",
+            )(toks, *bases)
+            part_other = swap_core(part_send)
+        if extra:
+            last_projected = swap_plane(outs[1], places - 1)
+
+    half = jax.ShapeDtypeStruct((2, share, rank), f32)
+    first_new, second_new, code = pl.pallas_call(
+        functools.partial(adam_kernel, places, share),
+        in_specs=[VMEM] * (places + 5),
+        out_specs=[VMEM] * 3,
+        out_shape=[half, half, jax.ShapeDtypeStruct((2, share, rank), bf16)],
+        compiler_params=pltpu.CompilerParams(vmem_limit_bytes=24 * MIB),
+        cost_estimate=pl.CostEstimate(
+            flops=6 * 2 * 2 * share * rank * places * 2 * group,
+            bytes_accessed=2 * share * rank * 20,
+            transcendentals=2 * share * rank,
+        ),
+        name="adam",
+    )(
+        messages[0],
+        part,
+        part_other,
+        *[messages[j] for j in range(1, places)],
+        last_projected,
+        first_moment.transpose(1, 0, 2),
+        second_moment.transpose(1, 0, 2),
+    )
+
+    codes = [swap_plane(code, j) for j in range(places - 1)]
+    relay = jnp.where(core == 0, codes[1], codes[2])
+    flips = [4 if i % 2 == 0 else 2 for i in range(n_dp)]
+    codes.append(lax.ppermute(relay, "dp", [(i, i ^ flips[i]) for i in range(n_dp)]))
+    moment_shape = jax.ShapeDtypeStruct((share, 2, rank), f32)
+    first_new, second_new = pl.pallas_call(
+        moments_kernel,
+        in_specs=[VMEM] * 2,
+        out_specs=[VMEM] * 2,
+        out_shape=[moment_shape] * 2,
+        compiler_params=pltpu.CompilerParams(vmem_limit_bytes=8 * MIB),
+        name="moments",
+    )(first_new, second_new)
+    master = pl.pallas_call(
+        functools.partial(load_master_kernel, places),
+        in_specs=[HBM],
+        out_specs=VMEM,
+        out_shape=pltpu.VMEM(master.shape, f32),
+        scratch_shapes=[pltpu.SemaphoreType.DMA((places,))],
+        compiler_params=pltpu.CompilerParams(vmem_limit_bytes=MIB),
+        cost_estimate=pl.CostEstimate(
+            flops=0, bytes_accessed=2 * 2 * ff * depth * 4, transcendentals=0
+        ),
+        name="load_master",
+    )(pltpu.with_memory_space_constraint(master, pltpu.HBM))
+    basis_twice = jnp.concatenate([basis.T, basis.T], axis=0)
+    master_new = None
+    for j in range(places):
+        for o, c in enumerate((codes[j], swap_core(codes[j]))):
+            kept = () if master_new is None else (master_new,)
+            master_new = pl.pallas_call(
+                functools.partial(lift_kernel, share, j, o),
+                in_specs=[VMEM] * 3 + [HBM] * len(kept),
+                out_specs=HBM,
+                out_shape=jax.ShapeDtypeStruct(master.shape, f32),
+                scratch_shapes=[
+                    pltpu.VMEM((2, share, depth), f32),
+                    pltpu.SemaphoreType.DMA((2,)),
+                ],
+                input_output_aliases={3: 0} if kept else {},
+                compiler_params=pltpu.CompilerParams(vmem_limit_bytes=16 * MIB),
+                cost_estimate=pl.CostEstimate(
+                    flops=2 * 2 * 2 * share * rank * depth,
+                    bytes_accessed=2 * 2 * share * depth * 4,
+                    transcendentals=4 * share * rank,
+                ),
+            )(c, basis_twice, master, *kept)
+    return master_new, first_new, second_new
+
+
+def plain_device(tokens, cotangent, weights, basis, master, first_moment, second_moment):
     highest = lax.Precision.HIGHEST
     group_tokens = lax.all_gather(tokens, "hid", axis=0, tiled=True)
     projected = jnp.dot(
@@ -52,7 +425,22 @@
     return (master_new, first_new, second_new)
 
 
+def power_of_two(n):
+    return n & (n - 1) == 0
+
+
 def solution(mesh):
+    n_dp, n_hid = mesh.shape["dp"], mesh.shape["hid"]
+
+    def on_device(tokens, cotangent, weights, *rest):
+        share = weights.shape[1] // n_dp
+        aligned = share % 16 == 0 and tokens.shape[0] % 16 == 0 and rest[0].shape[0] % 128 == 0
+        aligned = aligned and rest[0].shape[1] == (share // 128 + 1) * 128
+        few = n_dp == 8 and power_of_two(n_hid) and n_hid <= 8
+        if aligned and few:
+            return fast_device(n_dp, n_hid, tokens, cotangent, weights, *rest)
+        return plain_device(tokens, cotangent, weights, *rest)
+
     in_specs = (
         P(("dp", "hid"), None),
         P("dp", "hid"),

time: 156 us -> 69.7 us (0.45)
  waiting for transfers between devices: 85.9 us -> 17.6 us
  matrix products: 32.3 us -> 0 us
  Pallas kernels: 0 us -> 29.6 us
  starting transfers between devices: 0.12 us -> 20.1 us
  blocking collectives: 17.6 us -> 0 us
  between operations: 13.8 us -> 0.93 us
  other arithmetic: 4.27 us -> 0.06 us
    reduce_scatter x1 -> x0, waiting for transfers between devices: 51.6 us -> none  [on_device(): lax.psum_scatter(jnp.stack([gate_term, up_term], axis=1), 'dp', scatter_d...]
    all_gather x2 -> x0, waiting for transfers between devices: 33.6 us -> none  [the longest x1 33.5 us: on_device(): direction = lax.all_gather(direction_share, 'dp', axis=0, tiled=True)]
    dot_general x6 -> x0, matrix products: 32.3 us -> none  [the longest x1 9.06 us: on_device(): jnp.einsum('fwr,dr->wfd', direction, basis.astype(jnp.float32), precision...]
    pallas_call x0 -> x18, Pallas kernels: none -> 29.6 us  [the longest x8 10.7 us: fast_device(): pl.pallas_call(functools.partial(lift_kernel, share, j, o), in_specs=[VME...]
    ppermute x0 -> x23, starting transfers between devices: none -> 20.1 us  [the longest x22 19.3 us: swap(): return lax.ppermute(x, axis, [(i, i ^ flip) for i in range(n)])]
    ppermute x0 -> x23, waiting for transfers between devices: none -> 17.6 us  [the longest x22 16.2 us: swap(): return lax.ppermute(x, axis, [(i, i ^ flip) for i in range(n)])]
    all_gather x1 -> x0, blocking collectives: 17.6 us -> none  [on_device(): group_tokens = lax.all_gather(tokens, 'hid', axis=0, tiled=True)]
    another operation x1 -> x0, other arithmetic: 2.18 us -> none  [on_device(): jnp.stack([gate_term, up_term], axis=1)]
  transfers between devices with their start and end apart: 3 -> 23, of which waited for: 2 -> 8; matrix products, arithmetic and copies ran while one was open for 13% -> 0% of each run, Pallas kernels for 0% -> 38%
where the time goes in v1:
time: 69.7 us; the launch traced here: 69.5 us
  Pallas kernels  29.6 us (42%)
  starting transfers between devices  20.1 us (29%)
  waiting for transfers between devices  17.6 us (25%)
  local copies, waits for them, and re-layouts  1.18 us (2%)
  between operations  0.93 us (1%)
    ppermute x22, starting transfers between devices, swap(): return lax.ppermute(x, axis, [(i, i ^ flip) for i in range(n)])  19.3 us
    ppermute x22, waiting for transfers between devices, swap(): return lax.ppermute(x, axis, [(i, i ^ flip) for i in range(n)])  16.2 us
    pallas_call x8, Pallas kernels, fast_device(): pl.pallas_call(functools.partial(lift_kernel, share, j, o), in_specs=[VME...  10.7 us
    pallas_call x4, Pallas kernels, fast_device(): pl.pallas_call(functools.partial(grads_kernel, j, n_hid, rows, first, wit...  6.7 us
    pallas_call x1, Pallas kernels, fast_device(): pl.pallas_call(functools.partial(load_weights_kernel, share, places), in_...  5.58 us
    pallas_call x1, Pallas kernels, fast_device(): pl.pallas_call(functools.partial(load_master_kernel, places), in_specs=[H...  3.35 us
    pallas_call x1, Pallas kernels, fast_device(): pl.pallas_call(functools.partial(adam_kernel, places, share), in_specs=[V...  1.57 us
    ppermute x1, waiting for transfers between devices, fast_device(): lax.ppermute(relay, 'dp', [(i, i ^ flips[i]) for i in range(n_dp)])  1.44 us
  transfers between devices with their start and end apart: 23, of which 8 were waited for; matrix products, arithmetic and copies ran while one was open for 0% of the time, Pallas kernels for 38%

profile of v1, /device:TPU:0, one launch (start us, length us, event | category | flops | bytes accessed | tf_op | source)
XLA Modules:
  0.0 69.5 jit_solution(842977434225562758)
XLA Ops:
  0.6 3.1 %collective-permute-start = (bf16[16,4096]{1,0:T(8,128)(2,1)}, bf16[16,4096]{1,0:T(8,128)(2,1)S(1)}, u32[]{:S(2)}, u32[]{:S(2)}) collective-permute-start(bf16[16,4096]{1,0:T(8,128)(2,1)} %refs_0_.2), channel_id=1, source_target_pairs={{0,1},{1,0},{2,3},{3,2},{4,5},{5,4},{6,7},{7,6},{8,9},{9,8},{10,11... | collective-permute-start | bytes 393224 | tf_op jit(solution)/shard_map/ppermute | solution.py:227
  3.7 2.6 %collective-permute-start.1 = (bf16[16,4096]{1,0:T(8,128)(2,1)}, bf16[16,4096]{1,0:T(8,128)(2,1)S(1)}, u32[]{:S(2)}, u32[]{:S(2)}) collective-permute-start(bf16[16,4096]{1,0:T(8,128)(2,1)} %refs_0_.2), channel_id=1, source_target_pairs={{0,2},{1,3},{2,0},{3,1},{4,6},{5,7},{6,4},{7,5},{8,10},{9,11},{10,... | collective-permute-start | bytes 393224 | tf_op jit(solution)/shard_map/ppermute | solution.py:227
  9.0 2.7 %collective-permute-start.10 = (bf16[512,256]{1,0:T(8,128)(2,1)}, bf16[512,256]{1,0:T(8,128)(2,1)S(1)}, u32[]{:S(2)}, u32[]{:S(2)}) collective-permute-start(bf16[512,256]{1,0:T(8,128)(2,1)} %refs_0_.3), channel_id=1, source_target_pairs={{0,24},{4,28},{8,16},{12,20},{16,8},{20,12},{24,0},{28,4},{1,25},{... | collective-permute-start | bytes 786440 | tf_op jit(solution)/shard_map/ppermute | solution.py:227
  11.7 5.1 %collective-permute-done.1.refs_2_ = bf16[16,4096]{1,0:T(8,128)(2,1)S(1)} collective-permute-done((bf16[16,4096]{1,0:T(8,128)(2,1)}, bf16[16,4096]{1,0:T(8,128)(2,1)S(1)}, u32[]{:S(2)}, u32[]{:S(2)}) %collective-permute-start.1) | collective-permute-done | bytes 131104 | tf_op jit(solution)/shard_map/ppermute | solution.py:227
  16.8 1.5 %collective-permute-start.8 = (bf16[512,256]{1,0:T(8,128)(2,1)}, bf16[512,256]{1,0:T(8,128)(2,1)S(1)}, u32[]{:S(2)}, u32[]{:S(2)}) collective-permute-start(bf16[512,256]{1,0:T(8,128)(2,1)} %refs_0_.3), channel_id=1, source_target_pairs={{0,8},{4,12},{8,0},{12,4},{16,24},{20,28},{24,16},{28,20},{1,9},{5... | collective-permute-start | bytes 786440 | tf_op jit(solution)/shard_map/ppermute | solution.py:227
  18.3 1.5 %collective-permute-start.9 = (bf16[512,256]{1,0:T(8,128)(2,1)}, bf16[512,256]{1,0:T(8,128)(2,1)S(1)}, u32[]{:S(2)}, u32[]{:S(2)}) collective-permute-start(bf16[512,256]{1,0:T(8,128)(2,1)} %refs_0_.3), channel_id=1, source_target_pairs={{0,16},{4,20},{8,24},{12,28},{16,0},{20,4},{24,8},{28,12},{1,17},{... | collective-permute-start | bytes 786440 | tf_op jit(solution)/shard_map/ppermute | solution.py:227
  20.4 5.6 %load_weights.1.refs_8_.refs_1_ = bf16[4,2,240,4096]{3,2,1,0:T(8,128)(2,1)S(1)} custom-call(bf16[2,1920,4096]{2,1,0:T(8,128)(2,1)} %w_hbm.1), custom_call_target="tpu_custom_call" | custom-call | bytes 31457280 | tf_op jit(solution)/shard_map/load_weights/pallas_call | solution.py:254
  26.0 1.7 %shard_map.94 = (bf16[256,256]{1,0:T(8,128)(2,1)S(1)}, bf16[128,4096]{1,0:T(8,128)(2,1)S(1)}) custom-call(bf16[16,4096]{1,0:T(8,128)(2,1)S(1)} %copy-done.2, bf16[16,4096]{1,0:T(8,128)(2,1)S(1)} %collective-permute-done.refs_1_, bf16[16,4096]{1,0:T(8,128)(2,1)S(1)} %collective-permute-done.1.refs_2_, bf16[16,4096]{1,0:T(8,128)(2,1)S(1)} %collective-permute-done.2.refs_3_, ...), custom_call_target="tpu_custom_call" | custom-call | flops 503316480 | bytes 3932160 | tf_op jit(solution)/shard_map/pallas_call | solution.py:284
  29.5 1.8 %shard_map.97 = (bf16[400,256]{1,0:T(8,128)(2,1)S(1)}, bf16[144,256]{1,0:T(8,128)(2,1)S(1)}) custom-call(bf16[128,4096]{1,0:T(8,128)(2,1)S(1)} %get-tuple-element.18.refs_0_.tok, bf16[4,2,240,4096]{3,2,1,0:T(8,128)(2,1)S(1)} %load_weights.1.refs_8_.refs_1_, bf16[4,64,240]{2,1,0:T(8,128)(2,1)S(1)} %get-tuple-element.16.refs_9_.refs_2_, ...), custom_call_target="tpu_custom_call" | custom-call | flops 503316480 | bytes 3932160 | tf_op jit(solution)/shard_map/pallas_call | solution.py:284
  32.1 1.4 %collective-permute-start.15 = (bf16[144,256]{1,0:T(8,128)(2,1)S(1)}, bf16[144,256]{1,0:T(8,128)(2,1)S(1)}, u32[]{:S(2)}, u32[]{:S(2)}) collective-permute-start(bf16[144,256]{1,0:T(8,128)(2,1)S(1)} %get-tuple-element.23), channel_id=1, source_target_pairs={{0,24},{4,28},{8,16},{12,20},{16,8},{20,12},{24,0},{28,4},{1,25},{... | collective-permute-start | bytes 221192 | tf_op jit(solution)/shard_map/ppermute | solution.py:227
  33.5 1.8 %shard_map.96 = bf16[400,256]{1,0:T(8,128)(2,1)S(1)} custom-call(bf16[128,4096]{1,0:T(8,128)(2,1)S(1)} %get-tuple-element.18.refs_0_.tok, bf16[4,2,240,4096]{3,2,1,0:T(8,128)(2,1)S(1)} %load_weights.1.refs_8_.refs_1_, bf16[4,64,240]{2,1,0:T(8,128)(2,1)S(1)} %get-tuple-element.16.refs_9_.refs_2_, ...), custom_call_target="tpu_custom_call" | custom-call | flops 503316480 | bytes 3932160 | tf_op jit(solution)/shard_map/pallas_call | solution.py:284
  35.3 1.4 %collective-permute-start.12 = (bf16[400,256]{1,0:T(8,128)(2,1)S(1)}, bf16[400,256]{1,0:T(8,128)(2,1)S(1)}, u32[]{:S(2)}, u32[]{:S(2)}) collective-permute-start(bf16[400,256]{1,0:T(8,128)(2,1)S(1)} %shard_map.96), channel_id=1, source_target_pairs={{0,8},{4,12},{8,0},{12,4},{16,24},{20,28},{24,16},{28,20},{1,9},{5... | collective-permute-start | bytes 614408 | tf_op jit(solution)/shard_map/ppermute | solution.py:227
  36.8 1.5 %shard_map.95.own_grads = f32[2,128,240]{2,1,0:T(8,128)S(1)} custom-call(bf16[128,4096]{1,0:T(8,128)(2,1)S(1)} %get-tuple-element.18.refs_0_.tok, bf16[4,2,240,4096]{3,2,1,0:T(8,128)(2,1)S(1)} %load_weights.1.refs_8_.refs_1_, bf16[4,64,240]{2,1,0:T(8,128)(2,1)S(1)} %get-tuple-element.16.refs_9_.refs_2_, ...), custom_call_target="tpu_custom_call" | custom-call | flops 503316480 | bytes 3932160 | tf_op jit(solution)/shard_map/pallas_call | solution.py:284
  38.3 2.7 %collective-permute-done.13.refs_1_ = bf16[400,256]{1,0:T(8,128)(2,1)S(1)} collective-permute-done((bf16[400,256]{1,0:T(8,128)(2,1)S(1)}, bf16[400,256]{1,0:T(8,128)(2,1)S(1)}, u32[]{:S(2)}, u32[]{:S(2)}) %collective-permute-start.13) | collective-permute-done | bytes 204832 | tf_op jit(solution)/shard_map/ppermute | solution.py:227
  41.9 1.6 %adam.1 = (f32[2,240,256]{2,1,0:T(8,128)S(1)}, f32[2,240,256]{2,1,0:T(8,128)S(1)}, bf16[2,240,256]{2,1,0:T(8,128)(2,1)S(1)}) custom-call(f32[2,128,240]{2,1,0:T(8,128)S(1)} %shard_map.95.own_grads, f32[128,256]{1,0:T(8,128)S(1)} %get-tuple-element.19.refs_4_.part, f32[128,256]{1,0:T(8,128)S(1)} %collective-permute-done.11.refs_5_.part_other, ...), custom_call_target="tpu_custom_call" | custom-call | flops 754974720 | bytes 2457600 | tf_op jit(solution)/shard_map/adam/pallas_call | solution.py:318
  43.5 1.4 %collective-permute-start.16 = (bf16[2,240,256]{2,1,0:T(8,128)(2,1)S(1)}, bf16[2,240,256]{2,1,0:T(8,128)(2,1)S(1)}, u32[]{:S(2)}, u32[]{:S(2)}) collective-permute-start(bf16[2,240,256]{2,1,0:T(8,128)(2,1)S(1)} %get-tuple-element.24.refs_0_), channel_id=1, source_target_pairs={{0,8},{4,12},{8,0},{12,4},{16,24},{20,28},{24,16},{28,20},{1,9},{5... | collective-permute-start | bytes 737288 | tf_op jit(solution)/shard_map/ppermute | solution.py:227
  45.6 4.9 %collective-permute-done.16.refs_0_ = bf16[2,240,256]{2,1,0:T(8,128)(2,1)S(1)} collective-permute-done((bf16[2,240,256]{2,1,0:T(8,128)(2,1)S(1)}, bf16[2,240,256]{2,1,0:T(8,128)(2,1)S(1)}, u32[]{:S(2)}, u32[]{:S(2)}) %collective-permute-start.16) | collective-permute-done | bytes 245792 | tf_op jit(solution)/shard_map/ppermute | solution.py:227
  52.7 3.3 %load_master.1.refs_2_ = f32[2,1920,512]{2,1,0:T(8,128)S(1)} custom-call(f32[2,1920,512]{2,1,0:T(8,128)} %hbm.1), custom_call_target="tpu_custom_call" | custom-call | bytes 15728640 | tf_op jit(solution)/shard_map/load_master/pallas_call | solution.py:353
  56.0 1.4 %collective-permute-done.18.refs_0_ = bf16[2,240,256]{2,1,0:T(8,128)(2,1)S(1)} collective-permute-done((bf16[2,240,256]{2,1,0:T(8,128)(2,1)S(1)}, bf16[2,240,256]{2,1,0:T(8,128)(2,1)S(1)}, u32[]{:S(2)}, u32[]{:S(2)}) %collective-permute-start.18) | collective-permute-done | bytes 245792 | tf_op jit(solution)/shard_map/ppermute | solution.py:343
  60.0 1.3 %shard_map.99.refs_3_ = f32[2,1920,512]{2,1,0:T(8,128)} custom-call(bf16[2,240,256]{2,1,0:T(8,128)(2,1)S(1)} %collective-permute-done.22.refs_0_, bf16[512,512]{1,0:T(8,128)(2,1)S(1)} %pad_maximum_fusion.refs_1_, f32[2,1920,512]{2,1,0:T(8,128)S(1)} %load_master.1.refs_2_, f32[2,1920,512]{2,1,0:T(8,128)} %shard_map.98.refs_3_), custom_call_target="tpu_custom_call", output_to_operand_aliasing={{}: (3, {})} | custom-call | flops 251658240 | bytes 1966080 | tf_op jit(solution)/shard_map/pallas_call | solution.py:370
  61.4 1.3 %shard_map.100.refs_3_ = f32[2,1920,512]{2,1,0:T(8,128)} custom-call(bf16[2,240,256]{2,1,0:T(8,128)(2,1)S(1)} %collective-permute-done.16.refs_0_, bf16[512,512]{1,0:T(8,128)(2,1)S(1)} %pad_maximum_fusion.refs_1_, f32[2,1920,512]{2,1,0:T(8,128)S(1)} %load_master.1.refs_2_, f32[2,1920,512]{2,1,0:T(8,128)} %shard_map.99.refs_3_), custom_call_target="tpu_custom_call", output_to_operand_aliasing={{}: (3, {})} | custom-call | flops 251658240 | bytes 1966080 | tf_op jit(solution)/shard_map/pallas_call | solution.py:370
  64.1 1.3 %shard_map.102.refs_3_ = f32[2,1920,512]{2,1,0:T(8,128)} custom-call(bf16[2,240,256]{2,1,0:T(8,128)(2,1)S(1)} %collective-permute-done.17.refs_0_, bf16[512,512]{1,0:T(8,128)(2,1)S(1)} %pad_maximum_fusion.refs_1_, f32[2,1920,512]{2,1,0:T(8,128)S(1)} %load_master.1.refs_2_, f32[2,1920,512]{2,1,0:T(8,128)} %shard_map.101.refs_3_), custom_call_target="tpu_custom_call", output_to_operand_aliasing={{}: (3, {})} | custom-call | flops 251658240 | bytes 1966080 | tf_op jit(solution)/shard_map/pallas_call | solution.py:370
  66.8 1.3 %shard_map.104.refs_3_ = f32[2,1920,512]{2,1,0:T(8,128)} custom-call(bf16[2,240,256]{2,1,0:T(8,128)(2,1)S(1)} %collective-permute-done.18.refs_0_, bf16[512,512]{1,0:T(8,128)(2,1)S(1)} %pad_maximum_fusion.refs_1_, f32[2,1920,512]{2,1,0:T(8,128)S(1)} %load_master.1.refs_2_, f32[2,1920,512]{2,1,0:T(8,128)} %shard_map.103.refs_3_), custom_call_target="tpu_custom_call", output_to_operand_aliasing={{}: (3, {})} | custom-call | flops 251658240 | bytes 1966080 | tf_op jit(solution)/shard_map/pallas_call | solution.py:370
  68.2 1.3 %shard_map.105 = f32[2,1920,512]{2,1,0:T(8,128)} custom-call(bf16[2,240,256]{2,1,0:T(8,128)(2,1)S(1)} %collective-permute-done.19.refs_0_, bf16[512,512]{1,0:T(8,128)(2,1)S(1)} %pad_maximum_fusion.refs_1_, f32[2,1920,512]{2,1,0:T(8,128)S(1)} %load_master.1.refs_2_, f32[2,1920,512]{2,1,0:T(8,128)} %shard_map.104.refs_3_), custom_call_target="tpu_custom_call", output_to_operand_aliasing={{}: (3, {})} | custom-call | flops 251658240 | bytes 1966080 | tf_op jit(solution)/shard_map/pallas_call | solution.py:370
  (54 shorter events, 15.0 us)
Async XLA Ops:
  0.6 8.4 %collective-permute-start = (bf16[16,4096]{1,0:T(8,128)(2,1)}, bf16[16,4096]{1,0:T(8,128)(2,1)S(1)}, u32[]{:S(2)}, u32[]{:S(2)}) collective-permute-start(bf16[16,4096]{1,0:T(8,128)(2,1)} %refs_0_.2), channel_id=1, source_target_pairs={{0,1},{1,0},{2,3},{3,2},{4,5},{5,4},{6,7},{7,6},{8,9},{9,8},{10,11... | collective-permute-start | bytes 393224 | tf_op jit(solution)/shard_map/ppermute | solution.py:227
  3.7 13.1 %collective-permute-start.1 = (bf16[16,4096]{1,0:T(8,128)(2,1)}, bf16[16,4096]{1,0:T(8,128)(2,1)S(1)}, u32[]{:S(2)}, u32[]{:S(2)}) collective-permute-start(bf16[16,4096]{1,0:T(8,128)(2,1)} %refs_0_.2), channel_id=1, source_target_pairs={{0,2},{1,3},{2,0},{3,1},{4,6},{5,7},{6,4},{7,5},{8,10},{9,11},{10,... | collective-permute-start | bytes 393224 | tf_op jit(solution)/shard_map/ppermute | solution.py:227
  6.3 12.0 %collective-permute-start.2 = (bf16[16,4096]{1,0:T(8,128)(2,1)}, bf16[16,4096]{1,0:T(8,128)(2,1)S(1)}, u32[]{:S(2)}, u32[]{:S(2)}) collective-permute-start(bf16[16,4096]{1,0:T(8,128)(2,1)} %refs_0_.2), channel_id=1, source_target_pairs={{0,3},{1,2},{2,1},{3,0},{4,7},{5,6},{6,5},{7,4},{8,11},{9,10},{10,... | collective-permute-start | bytes 393224 | tf_op jit(solution)/shard_map/ppermute | solution.py:227
  7.5 18.5 %copy-start.2 = (bf16[16,4096]{1,0:T(8,128)(2,1)S(1)}, bf16[16,4096]{1,0:T(8,128)(2,1)}, u32[]{:S(2)}) copy-start(bf16[16,4096]{1,0:T(8,128)(2,1)} %refs_0_.2) | copy-start | bytes 393220
  7.5 1.6 %collective-permute-start.7 = (bf16[4,64,240]{2,1,0:T(8,128)(2,1)S(1)}, bf16[4,64,240]{2,1,0:T(8,128)(2,1)S(1)}, u32[]{:S(2)}, u32[]{:S(2)}) collective-permute-start(bf16[4,64,240]{2,1,0:T(8,128)(2,1)S(1)} %get-tuple-element.17), channel_id=1, source_target_pairs={{0,4},{4,0},{8,12},{12,8},{16,20},{20,16},{24,28},{28,24},{1,5},{5... | collective-permute-start | bytes 368648 | tf_op jit(solution)/shard_map/ppermute | solution.py:227
  7.6 12.3 %collective-permute-start.3 = (bf16[16,4096]{1,0:T(8,128)(2,1)}, bf16[16,4096]{1,0:T(8,128)(2,1)S(1)}, u32[]{:S(2)}, u32[]{:S(2)}) collective-permute-start(bf16[16,4096]{1,0:T(8,128)(2,1)} %refs_0_.2), channel_id=1, source_target_pairs={{0,4},{4,0},{8,12},{12,8},{16,20},{20,16},{24,28},{28,24},{1,5},{5... | collective-permute-start | bytes 393224 | tf_op jit(solution)/shard_map/ppermute | solution.py:227
  9.0 10.8 %collective-permute-start.4 = (bf16[16,4096]{1,0:T(8,128)(2,1)S(1)}, bf16[16,4096]{1,0:T(8,128)(2,1)S(1)}, u32[]{:S(2)}, u32[]{:S(2)}) collective-permute-start(bf16[16,4096]{1,0:T(8,128)(2,1)S(1)} %collective-permute-done.refs_1_), channel_id=1, source_target_pairs={{0,4},{4,0},{8,12},{12,8},{16,20},{20,16},{24,28},{28,24},{1,5},{5... | collective-permute-start | bytes 393224 | tf_op jit(solution)/shard_map/ppermute | solution.py:227
  9.0 18.7 %collective-permute-start.10 = (bf16[512,256]{1,0:T(8,128)(2,1)}, bf16[512,256]{1,0:T(8,128)(2,1)S(1)}, u32[]{:S(2)}, u32[]{:S(2)}) collective-permute-start(bf16[512,256]{1,0:T(8,128)(2,1)} %refs_0_.3), channel_id=1, source_target_pairs={{0,24},{4,28},{8,16},{12,20},{16,8},{20,12},{24,0},{28,4},{1,25},{... | collective-permute-start | bytes 786440 | tf_op jit(solution)/shard_map/ppermute | solution.py:227
  16.8 10.9 %collective-permute-start.8 = (bf16[512,256]{1,0:T(8,128)(2,1)}, bf16[512,256]{1,0:T(8,128)(2,1)S(1)}, u32[]{:S(2)}, u32[]{:S(2)}) collective-permute-start(bf16[512,256]{1,0:T(8,128)(2,1)} %refs_0_.3), channel_id=1, source_target_pairs={{0,8},{4,12},{8,0},{12,4},{16,24},{20,28},{24,16},{28,20},{1,9},{5... | collective-permute-start | bytes 786440 | tf_op jit(solution)/shard_map/ppermute | solution.py:227
  18.3 9.4 %collective-permute-start.9 = (bf16[512,256]{1,0:T(8,128)(2,1)}, bf16[512,256]{1,0:T(8,128)(2,1)S(1)}, u32[]{:S(2)}, u32[]{:S(2)}) collective-permute-start(bf16[512,256]{1,0:T(8,128)(2,1)} %refs_0_.3), channel_id=1, source_target_pairs={{0,16},{4,20},{8,24},{12,28},{16,0},{20,4},{24,8},{28,12},{1,17},{... | collective-permute-start | bytes 786440 | tf_op jit(solution)/shard_map/ppermute | solution.py:227
  19.9 6.1 %collective-permute-start.5 = (bf16[16,4096]{1,0:T(8,128)(2,1)S(1)}, bf16[16,4096]{1,0:T(8,128)(2,1)S(1)}, u32[]{:S(2)}, u32[]{:S(2)}) collective-permute-start(bf16[16,4096]{1,0:T(8,128)(2,1)S(1)} %collective-permute-done.1.refs_2_), channel_id=1, source_target_pairs={{0,4},{4,0},{8,12},{12,8},{16,20},{20,16},{24,28},{28,24},{1,5},{5... | collective-permute-start | bytes 393224 | tf_op jit(solution)/shard_map/ppermute | solution.py:227
  19.9 6.1 %collective-permute-start.6 = (bf16[16,4096]{1,0:T(8,128)(2,1)S(1)}, bf16[16,4096]{1,0:T(8,128)(2,1)S(1)}, u32[]{:S(2)}, u32[]{:S(2)}) collective-permute-start(bf16[16,4096]{1,0:T(8,128)(2,1)S(1)} %collective-permute-done.2.refs_3_), channel_id=1, source_target_pairs={{0,4},{4,0},{8,12},{12,8},{16,20},{20,16},{24,28},{28,24},{1,5},{5... | collective-permute-start | bytes 393224 | tf_op jit(solution)/shard_map/ppermute | solution.py:227
  28.1 1.4 %collective-permute-start.11 = (f32[128,256]{1,0:T(8,128)S(1)}, f32[128,256]{1,0:T(8,128)S(1)}, u32[]{:S(2)}, u32[]{:S(2)}) collective-permute-start(f32[128,256]{1,0:T(8,128)S(1)} %get-tuple-element.20), channel_id=1, source_target_pairs={{0,4},{4,0},{8,12},{12,8},{16,20},{20,16},{24,28},{28,24},{1,5},{5... | collective-permute-start | bytes 393224 | tf_op jit(solution)/shard_map/ppermute | solution.py:227
  28.2 10.0 %collective-permute-start.14 = (bf16[256,256]{1,0:T(8,128)(2,1)S(1)}, bf16[256,256]{1,0:T(8,128)(2,1)S(1)}, u32[]{:S(2)}, u32[]{:S(2)}) collective-permute-start(bf16[256,256]{1,0:T(8,128)(2,1)S(1)} %get-tuple-element.22), channel_id=1, source_target_pairs={{0,24},{4,28},{8,16},{12,20},{16,8},{20,12},{24,0},{28,4},{1,25},{... | collective-permute-start | bytes 393224 | tf_op jit(solution)/shard_map/ppermute | solution.py:227
  31.3 9.7 %collective-permute-start.13 = (bf16[400,256]{1,0:T(8,128)(2,1)S(1)}, bf16[400,256]{1,0:T(8,128)(2,1)S(1)}, u32[]{:S(2)}, u32[]{:S(2)}) collective-permute-start(bf16[400,256]{1,0:T(8,128)(2,1)S(1)} %get-tuple-element.21), channel_id=1, source_target_pairs={{0,16},{4,20},{8,24},{12,28},{16,0},{20,4},{24,8},{28,12},{1,17},{... | collective-permute-start | bytes 614408 | tf_op jit(solution)/shard_map/ppermute | solution.py:227
  32.1 6.2 %collective-permute-start.15 = (bf16[144,256]{1,0:T(8,128)(2,1)S(1)}, bf16[144,256]{1,0:T(8,128)(2,1)S(1)}, u32[]{:S(2)}, u32[]{:S(2)}) collective-permute-start(bf16[144,256]{1,0:T(8,128)(2,1)S(1)} %get-tuple-element.23), channel_id=1, source_target_pairs={{0,24},{4,28},{8,16},{12,20},{16,8},{20,12},{24,0},{28,4},{1,25},{... | collective-permute-start | bytes 221192 | tf_op jit(solution)/shard_map/ppermute | solution.py:227
  35.3 6.6 %collective-permute-start.12 = (bf16[400,256]{1,0:T(8,128)(2,1)S(1)}, bf16[400,256]{1,0:T(8,128)(2,1)S(1)}, u32[]{:S(2)}, u32[]{:S(2)}) collective-permute-start(bf16[400,256]{1,0:T(8,128)(2,1)S(1)} %shard_map.96), channel_id=1, source_target_pairs={{0,8},{4,12},{8,0},{12,4},{16,24},{20,28},{24,16},{28,20},{1,9},{5... | collective-permute-start | bytes 614408 | tf_op jit(solution)/shard_map/ppermute | solution.py:227
  43.5 7.0 %collective-permute-start.16 = (bf16[2,240,256]{2,1,0:T(8,128)(2,1)S(1)}, bf16[2,240,256]{2,1,0:T(8,128)(2,1)S(1)}, u32[]{:S(2)}, u32[]{:S(2)}) collective-permute-start(bf16[2,240,256]{2,1,0:T(8,128)(2,1)S(1)} %get-tuple-element.24.refs_0_), channel_id=1, source_target_pairs={{0,8},{4,12},{8,0},{12,4},{16,24},{20,28},{24,16},{28,20},{1,9},{5... | collective-permute-start | bytes 737288 | tf_op jit(solution)/shard_map/ppermute | solution.py:227
  44.9 6.3 %collective-permute-start.17 = (bf16[2,240,256]{2,1,0:T(8,128)(2,1)S(1)}, bf16[2,240,256]{2,1,0:T(8,128)(2,1)S(1)}, u32[]{:S(2)}, u32[]{:S(2)}) collective-permute-start(bf16[2,240,256]{2,1,0:T(8,128)(2,1)S(1)} %get-tuple-element.24.refs_0_), channel_id=1, source_target_pairs={{0,16},{4,20},{8,24},{12,28},{16,0},{20,4},{24,8},{28,12},{1,17},{... | collective-permute-start | bytes 737288 | tf_op jit(solution)/shard_map/ppermute | solution.py:227
  51.2 6.3 %collective-permute-start.18 = (bf16[2,240,256]{2,1,0:T(8,128)(2,1)S(1)}, bf16[2,240,256]{2,1,0:T(8,128)(2,1)S(1)}, u32[]{:S(2)}, u32[]{:S(2)}) collective-permute-start(bf16[2,240,256]{2,1,0:T(8,128)(2,1)S(1)} %broadcast_select_fusion), channel_id=1, source_target_pairs={{0,16},{4,12},{8,24},{12,4},{16,0},{20,28},{24,8},{28,20},{1,17},{... | collective-permute-start | bytes 737288 | tf_op jit(solution)/shard_map/ppermute | solution.py:343
  52.0 8.0 %collective-permute-start.22 = (bf16[2,240,256]{2,1,0:T(8,128)(2,1)S(1)}, bf16[2,240,256]{2,1,0:T(8,128)(2,1)S(1)}, u32[]{:S(2)}, u32[]{:S(2)}) collective-permute-start(bf16[2,240,256]{2,1,0:T(8,128)(2,1)S(1)} %get-tuple-element.24.refs_0_), channel_id=1, source_target_pairs={{0,4},{4,0},{8,12},{12,8},{16,20},{20,16},{24,28},{28,24},{1,5},{5... | collective-permute-start | bytes 737288 | tf_op jit(solution)/shard_map/ppermute | solution.py:227
  52.0 10.7 %collective-permute-start.21 = (bf16[2,240,256]{2,1,0:T(8,128)(2,1)S(1)}, bf16[2,240,256]{2,1,0:T(8,128)(2,1)S(1)}, u32[]{:S(2)}, u32[]{:S(2)}) collective-permute-start(bf16[2,240,256]{2,1,0:T(8,128)(2,1)S(1)} %collective-permute-done.16.refs_0_), channel_id=1, source_target_pairs={{0,4},{4,0},{8,12},{12,8},{16,20},{20,16},{24,28},{28,24},{1,5},{5... | collective-permute-start | bytes 737288 | tf_op jit(solution)/shard_map/ppermute | solution.py:227
  52.5 12.9 %collective-permute-start.20 = (bf16[2,240,256]{2,1,0:T(8,128)(2,1)S(1)}, bf16[2,240,256]{2,1,0:T(8,128)(2,1)S(1)}, u32[]{:S(2)}, u32[]{:S(2)}) collective-permute-start(bf16[2,240,256]{2,1,0:T(8,128)(2,1)S(1)} %collective-permute-done.17.refs_0_), channel_id=1, source_target_pairs={{0,4},{4,0},{8,12},{12,8},{16,20},{20,16},{24,28},{28,24},{1,5},{5... | collective-permute-start | bytes 737288 | tf_op jit(solution)/shard_map/ppermute | solution.py:227
  57.5 10.7 %collective-permute-start.19 = (bf16[2,240,256]{2,1,0:T(8,128)(2,1)S(1)}, bf16[2,240,256]{2,1,0:T(8,128)(2,1)S(1)}, u32[]{:S(2)}, u32[]{:S(2)}) collective-permute-start(bf16[2,240,256]{2,1,0:T(8,128)(2,1)S(1)} %collective-permute-done.18.refs_0_), channel_id=1, source_target_pairs={{0,4},{4,0},{8,12},{12,8},{16,20},{20,16},{24,28},{28,24},{1,5},{5... | collective-permute-start | bytes 737288 | tf_op jit(solution)/shard_map/ppermute | solution.py:227
  (4 other events, 11.9 us)

commit v2 on v1

--- a/solution.py
+++ b/solution.py
@@ -21,6 +21,7 @@
 
 VMEM = pl.BlockSpec(memory_space=pltpu.VMEM)
 HBM = pl.BlockSpec(memory_space=pltpu.HBM)
+SMALL = pl.CostEstimate(flops=1000, bytes_accessed=1000, transcendentals=0)
 MIB = 1 << 20
 
 
@@ -43,8 +44,7 @@
 
 def decode(y, inverse_scale, squarings):
     a = jnp.abs(y)
-    root = jnp.exp(jnp.log(jnp.where(a == 0, 1.0, a)) * 0.5**squarings) * inverse_scale
-    root = jnp.where(a == 0, 0.0, root)
+    root = jnp.exp(jnp.log(a) * 0.5**squarings) * inverse_scale
     return jnp.where(y < 0, -root, root)
 
 
@@ -97,16 +97,13 @@
     out_send[half:] = total[:half]
 
 
-def grads_kernel(j, n_hid, rows, with_tokens, with_projected, extra_projected, *refs):
-    refs = list(refs)
+def grads_kernel(j, n_hid, rows, with_tokens, *refs):
     pieces = 2 * n_hid if with_tokens else 1
     toks, (w, cot_own, cot_other) = refs[:pieces], refs[pieces : pieces + 3]
-    refs = refs[pieces + 3 :]
-    part, part_other = (refs.pop(0), refs.pop(0)) if with_projected else (None, None)
-    out = refs[0]
+    out = refs[pieces + 3]
     tok = toks[0]
     if with_tokens:
-        tok = refs[1]
+        tok = refs[-1]
         for i, t in enumerate(toks):
             tok[i * rows : (i + 1) * rows] = t[...]
     contract = (((1,), (1,)), ((), ()))
@@ -133,18 +130,23 @@
         here = slice(k * n_tok, (k + 1) * n_tok)
         out[here, :share] = encode(terms[k], wide, code_squarings)
         out[here, share:] = jnp.broadcast_to(scale, (n_tok, out.shape[1] - share))
-    if with_projected:
-        projected = part[...] + part_other[...]
-        scale = scale_for(projected)
-        coded = encode(projected, scale.astype(jnp.float32), code_squarings)
-        for ref, top in [(out, 2 * n_tok)] + ([(refs[1], 0)] if extra_projected else []):
-            ref[top : top + n_tok] = coded
-            ref[top + n_tok :] = jnp.broadcast_to(scale, (ref.shape[0] - top - n_tok, ref.shape[1]))
+
+
+def code_projected_kernel(part, part_other, basis, out, basis_twice):
+    n_tok = part.shape[0]
+    projected = part[...] + part_other[...]
+    scale = scale_for(projected)
+    out[:n_tok] = encode(projected, scale.astype(jnp.float32), code_squarings)
+    out[n_tok:] = jnp.broadcast_to(scale, (out.shape[0] - n_tok, out.shape[1]))
+    turned = basis[...].T
+    rank = turned.shape[0]
+    basis_twice[:rank] = turned
+    basis_twice[rank:] = turned
 
 
 def adam_kernel(places, share, own_grads, part, part_other, *refs):
-    messages = refs[: places - 1]
-    last_projected, first, second, first_new, second_new, code = refs[places - 1 :]
+    messages, coded = refs[: places - 1], refs[places - 1 : 2 * places - 2]
+    first, second, first_new, second_new, code = refs[2 * places - 2 :]
     n_tok = part.shape[0]
     dot = functools.partial(
         lax.dot_general,
@@ -152,10 +154,9 @@
         preferred_element_type=jnp.float32,
     )
     projs = [part[...] + part_other[...]]
-    for i, m in enumerate(messages):
-        ref, top = (m, 2 * n_tok) if i < places - 2 else (last_projected, 0)
-        values = ref[top : top + n_tok].astype(jnp.float32)
-        scale = ref[top + n_tok : top + n_tok + 1, :].astype(jnp.float32)
+    for ref in coded:
+        values = ref[:n_tok].astype(jnp.float32)
+        scale = ref[n_tok : n_tok + 1, :].astype(jnp.float32)
         projs.append(decode(values, 1.0 / scale, code_squarings))
     p_high, p_low = split(jnp.concatenate(projs, axis=0))
     for k in range(2):
@@ -173,42 +174,38 @@
         code[k] = encode(m / (jnp.sqrt(v) + adam_epsilon), code_scale, code_scale_squarings)
 
 
+def moments_in_kernel(first, second, first_out, second_out):
+    for k in range(2):
+        first_out[k] = first[:, k]
+        second_out[k] = second[:, k]
+
+
 def moments_kernel(first, second, first_out, second_out):
     for k in range(2):
         first_out[:, k] = first[k]
         second_out[:, k] = second[k]
 
 
-def load_master_kernel(pieces, hbm, out, sem):
-    rows = out.shape[1] // pieces
-    copies = []
-    for i in range(pieces):
-        at = (slice(None), pl.ds(i * rows, rows))
-        copies.append(pltpu.make_async_copy(hbm.at[at], out.at[at], sem.at[i]))
-    for c in copies:
-        c.start()
-    for c in copies:
-        c.wait()
-
-
-def lift_kernel(share, j, other, *refs):
-    codes, basis, master = refs[:3]
+def lift_kernel(share, pieces, *refs):
+    codes = refs[: len(pieces)]
+    basis, master = refs[len(pieces) : len(pieces) + 2]
     out, o_buf, sem = refs[-3:]
     core = lax.rem(lax.axis_index("dp"), 2)
     plane = lax.div(lax.axis_index("dp"), 2)
-    who = 2 * jnp.bitwise_xor(plane, j) + jnp.bitwise_xor(core, other)
-    row = pl.ds(pl.multiple_of(who * share, 16), share)
     copies = []
     for k in range(2):
-        values = codes[k].astype(jnp.float32)
+        values = jnp.concatenate([c[k] for c in codes], axis=0).astype(jnp.float32)
         terms = split(decode(values, step_size / code_scale, code_scale_squarings))
         lifted = jnp.dot(
             jnp.concatenate(terms, axis=1), basis[...], preferred_element_type=jnp.float32
         )
-        o_buf[k] = master[k, row, :] - lifted
-        c = pltpu.make_async_copy(o_buf.at[k], out.at[k, row], sem.at[k])
-        c.start()
-        copies.append(c)
+        for i, (j, other) in enumerate(pieces):
+            who = 2 * jnp.bitwise_xor(plane, j) + jnp.bitwise_xor(core, other)
+            row = pl.ds(pl.multiple_of(who * share, 16), share)
+            o_buf[k, i] = master[k, row, :] - lifted[i * share : (i + 1) * share]
+            c = pltpu.make_async_copy(o_buf.at[k, i], out.at[k, row], sem.at[k, i])
+            c.start()
+            copies.append(c)
     for c in copies:
         c.wait()
 
@@ -235,8 +232,6 @@
     def swap_core(x):
         return swap(x, "dp", 1)
 
-    core = lax.rem(lax.axis_index("dp"), 2)
-
     own = [tokens] + [swap_hid(tokens, k) for k in range(n_hid - 1, 0, -1)][::-1]
     bases = [basis] + [swap_plane(basis, j) for j in range(1, places)]
 
@@ -247,6 +242,7 @@
         out_specs=[VMEM] * 2,
         out_shape=[cot_shape] * 2,
         compiler_params=pltpu.CompilerParams(vmem_limit_bytes=4 * MIB),
+        cost_estimate=SMALL,
         name="cotangents",
     )(cotangent)
     cot_other = swap_core(cot_send)
@@ -265,82 +261,92 @@
     )(pltpu.with_memory_space_constraint(weights, pltpu.HBM))
 
     other = [swap_core(t) for t in own]
-    messages, part, part_other = {}, None, None
+    messages = {}
     n_tok, spare = 2 * group, 16
-    for j in [places - 1, 0] + list(range(places - 2, 0, -1)):
-        first, extra = j == places - 1, j == places - 2
-        with_projected = bool(j) and not first
+    for j in list(range(places - 1, -1, -1)):
+        first = j == places - 1
         ins = (own + other if first else [toks]) + [held, cot_own, cot_other]
-        ins += [part, part_other] if with_projected else []
-        if not j:
+        if j:
+            shapes = [jax.ShapeDtypeStruct((2 * n_tok, rank), bf16)]
+        else:
             shapes = [jax.ShapeDtypeStruct((2, n_tok, share), f32)]
-        else:
-            depth_of = 2 * n_tok + (n_tok + spare if with_projected else 0)
-            shapes = [jax.ShapeDtypeStruct((depth_of, rank), bf16)]
         if first:
             shapes.append(jax.ShapeDtypeStruct((n_tok, width), bf16))
-        if extra:
-            shapes.append(jax.ShapeDtypeStruct((n_tok + spare, rank), bf16))
         outs = pl.pallas_call(
-            functools.partial(grads_kernel, j, n_hid, rows, first, with_projected, extra),
+            functools.partial(grads_kernel, j, n_hid, rows, first),
             in_specs=[VMEM] * len(ins),
             out_specs=[VMEM] * len(shapes),
             out_shape=shapes,
-            compiler_params=pltpu.CompilerParams(vmem_limit_bytes=16 * MIB),
+            compiler_params=pltpu.CompilerParams(vmem_limit_bytes=6 * MIB),
             cost_estimate=pl.CostEstimate(
                 flops=2 * n_tok * 2 * share * width,
                 bytes_accessed=2 * share * width * 2,
                 transcendentals=n_tok * share,
-            ),
+            )
+            if j
+            else SMALL,
         )(*ins)
         messages[j] = swap_plane(outs[0], j)
         if first:
             toks = outs[1]
-            part_shape = jax.ShapeDtypeStruct((n_tok, rank), f32)
-            part, part_send = pl.pallas_call(
-                functools.partial(project_kernel, places),
-                in_specs=[VMEM] * (1 + places),
-                out_specs=[VMEM] * 2,
-                out_shape=[part_shape] * 2,
-                compiler_params=pltpu.CompilerParams(vmem_limit_bytes=16 * MIB),
-                cost_estimate=pl.CostEstimate(
-                    flops=2 * n_tok * places * depth * rank,
-                    bytes_accessed=n_tok * width * 2,
-                    transcendentals=0,
-                ),
-                name="project",
-            )(toks, *bases)
-            part_other = swap_core(part_send)
-        if extra:
-            last_projected = swap_plane(outs[1], places - 1)
+
+    part_shape = jax.ShapeDtypeStruct((n_tok, rank), f32)
+    part, part_send = pl.pallas_call(
+        functools.partial(project_kernel, places),
+        in_specs=[VMEM] * (1 + places),
+        out_specs=[VMEM] * 2,
+        out_shape=[part_shape] * 2,
+        compiler_params=pltpu.CompilerParams(vmem_limit_bytes=6 * MIB),
+        cost_estimate=pl.CostEstimate(
+            flops=2 * n_tok * places * depth * rank,
+            bytes_accessed=n_tok * width * 2,
+            transcendentals=0,
+        ),
+        name="project",
+    )(toks, *bases)
+    part_other = swap_core(part_send)
+    coded, basis_twice = pl.pallas_call(
+        code_projected_kernel,
+        in_specs=[VMEM] * 3,
+        out_specs=[VMEM] * 2,
+        out_shape=[
+            jax.ShapeDtypeStruct((n_tok + spare, rank), bf16),
+            jax.ShapeDtypeStruct((2 * rank, depth), bf16),
+        ],
+        compiler_params=pltpu.CompilerParams(vmem_limit_bytes=8 * MIB),
+        cost_estimate=SMALL,
+        name="code_projected",
+    )(part, part_other, basis)
 
     half = jax.ShapeDtypeStruct((2, share, rank), f32)
+    first_held, second_held = pl.pallas_call(
+        moments_in_kernel,
+        in_specs=[VMEM] * 2,
+        out_specs=[VMEM] * 2,
+        out_shape=[half] * 2,
+        compiler_params=pltpu.CompilerParams(vmem_limit_bytes=8 * MIB),
+        cost_estimate=SMALL,
+        name="moments_in",
+    )(first_moment, second_moment)
     first_new, second_new, code = pl.pallas_call(
         functools.partial(adam_kernel, places, share),
-        in_specs=[VMEM] * (places + 5),
+        in_specs=[VMEM] * (2 * places + 3),
         out_specs=[VMEM] * 3,
         out_shape=[half, half, jax.ShapeDtypeStruct((2, share, rank), bf16)],
-        compiler_params=pltpu.CompilerParams(vmem_limit_bytes=24 * MIB),
-        cost_estimate=pl.CostEstimate(
-            flops=6 * 2 * 2 * share * rank * places * 2 * group,
-            bytes_accessed=2 * share * rank * 20,
-            transcendentals=2 * share * rank,
-        ),
+        compiler_params=pltpu.CompilerParams(vmem_limit_bytes=12 * MIB),
+        cost_estimate=SMALL,
         name="adam",
     )(
         messages[0],
         part,
         part_other,
         *[messages[j] for j in range(1, places)],
-        last_projected,
-        first_moment.transpose(1, 0, 2),
-        second_moment.transpose(1, 0, 2),
-    )
-
-    codes = [swap_plane(code, j) for j in range(places - 1)]
-    relay = jnp.where(core == 0, codes[1], codes[2])
-    flips = [4 if i % 2 == 0 else 2 for i in range(n_dp)]
-    codes.append(lax.ppermute(relay, "dp", [(i, i ^ flips[i]) for i in range(n_dp)]))
+        *[swap_plane(coded, j) for j in range(1, places)],
+        first_held,
+        second_held,
+    )
+
+    codes = [swap_plane(code, j) for j in range(places)]
     moment_shape = jax.ShapeDtypeStruct((share, 2, rank), f32)
     first_new, second_new = pl.pallas_call(
         moments_kernel,
@@ -348,42 +354,32 @@
         out_specs=[VMEM] * 2,
         out_shape=[moment_shape] * 2,
         compiler_params=pltpu.CompilerParams(vmem_limit_bytes=8 * MIB),
+        cost_estimate=SMALL,
         name="moments",
     )(first_new, second_new)
-    master = pl.pallas_call(
-        functools.partial(load_master_kernel, places),
-        in_specs=[HBM],
-        out_specs=VMEM,
-        out_shape=pltpu.VMEM(master.shape, f32),
-        scratch_shapes=[pltpu.SemaphoreType.DMA((places,))],
-        compiler_params=pltpu.CompilerParams(vmem_limit_bytes=MIB),
-        cost_estimate=pl.CostEstimate(
-            flops=0, bytes_accessed=2 * 2 * ff * depth * 4, transcendentals=0
-        ),
-        name="load_master",
-    )(pltpu.with_memory_space_constraint(master, pltpu.HBM))
-    basis_twice = jnp.concatenate([basis.T, basis.T], axis=0)
+    pieces = {(j, 0): codes[j] for j in range(places)}
+    pieces.update({(j, 1): swap_core(codes[j]) for j in range(places)})
     master_new = None
-    for j in range(places):
-        for o, c in enumerate((codes[j], swap_core(codes[j]))):
-            kept = () if master_new is None else (master_new,)
-            master_new = pl.pallas_call(
-                functools.partial(lift_kernel, share, j, o),
-                in_specs=[VMEM] * 3 + [HBM] * len(kept),
-                out_specs=HBM,
-                out_shape=jax.ShapeDtypeStruct(master.shape, f32),
-                scratch_shapes=[
-                    pltpu.VMEM((2, share, depth), f32),
-                    pltpu.SemaphoreType.DMA((2,)),
-                ],
-                input_output_aliases={3: 0} if kept else {},
-                compiler_params=pltpu.CompilerParams(vmem_limit_bytes=16 * MIB),
-                cost_estimate=pl.CostEstimate(
-                    flops=2 * 2 * 2 * share * rank * depth,
-                    bytes_accessed=2 * 2 * share * depth * 4,
-                    transcendentals=4 * share * rank,
-                ),
-            )(c, basis_twice, master, *kept)
+    for some in lift_groups(places):
+        kept = () if master_new is None else (master_new,)
+        ins = [pieces[at] for at in some] + [basis_twice, master]
+        master_new = pl.pallas_call(
+            functools.partial(lift_kernel, share, some),
+            in_specs=[VMEM] * len(ins) + [HBM] * len(kept),
+            out_specs=HBM,
+            out_shape=jax.ShapeDtypeStruct(master.shape, f32),
+            scratch_shapes=[
+                pltpu.VMEM((2, len(some), share, depth), f32),
+                pltpu.SemaphoreType.DMA((2, len(some))),
+            ],
+            input_output_aliases={len(ins): 0} if kept else {},
+            compiler_params=pltpu.CompilerParams(vmem_limit_bytes=12 * MIB),
+            cost_estimate=pl.CostEstimate(
+                flops=2 * 2 * 2 * len(some) * share * rank * depth,
+                bytes_accessed=2 * 2 * len(some) * share * depth * 4,
+                transcendentals=4 * len(some) * share * rank,
+            ),
+        )(*ins, *kept)
     return master_new, first_new, second_new
 
 
@@ -423,6 +419,11 @@
     lifted = jnp.einsum("fwr,dr->wfd", direction, basis.astype(jnp.float32), precision=highest)
     master_new = master - step_size * lifted
     return (master_new, first_new, second_new)
+
+
+def lift_groups(places):
+    groups = [[(j, 0), (j, 1)] for j in range(places - 2)]
+    return groups + [[(j, other) for j in (places - 2, places - 1)] for other in range(2)]
 
 
 def power_of_two(n):

time: 69.7 us -> 67.9 us (0.974)
  Pallas kernels: 29.6 us -> 23 us
  starting transfers between devices: 20.1 us -> 23.9 us
  waiting for transfers between devices: 17.6 us -> 19 us
    pallas_call x13 -> x10, Pallas kernels: 20.8 us -> 14.3 us  [the longest x4 7.19 us: fast_device(): pl.pallas_call(functools.partial(lift_kernel, share, some), in_specs=[VME...]
    ppermute x22 -> x25, starting transfers between devices: 19.3 us -> 23.9 us  [swap(): return lax.ppermute(x, axis, [(i, i ^ flip) for i in range(n)])]
    ppermute x22 -> x25, waiting for transfers between devices: 16.2 us -> 19 us  [swap(): return lax.ppermute(x, axis, [(i, i ^ flip) for i in range(n)])]
    ppermute x1 -> x0, waiting for transfers between devices: 1.44 us -> none  [fast_device(): lax.ppermute(relay, 'dp', [(i, i ^ flips[i]) for i in range(n_dp)])]
    ppermute x1 -> x0, starting transfers between devices: 0.81 us -> none  [fast_device(): lax.ppermute(relay, 'dp', [(i, i ^ flips[i]) for i in range(n_dp)])]
  transfers between devices with their start and end apart: 23 -> 25, of which waited for: 8 -> 7; matrix products, arithmetic and copies ran while one was open for 0% -> 0% of each run, Pallas kernels for 38% -> 29%
where the time goes in v2:
time: 67.9 us; the launch traced here: 67.7 us
  starting transfers between devices  23.9 us (35%)
  Pallas kernels  23 us (34%)
  waiting for transfers between devices  19 us (28%)
  local copies, waits for them, and re-layouts  0.98 us (1%)
  between operations  0.9 us (1%)
    ppermute x25, starting transfers between devices, swap(): return lax.ppermute(x, axis, [(i, i ^ flip) for i in range(n)])  23.9 us
    ppermute x25, waiting for transfers between devices, swap(): return lax.ppermute(x, axis, [(i, i ^ flip) for i in range(n)])  19 us
    pallas_call x4, Pallas kernels, fast_device(): pl.pallas_call(functools.partial(lift_kernel, share, some), in_specs=[VME...  7.19 us
    pallas_call x4, Pallas kernels, fast_device(): pl.pallas_call(functools.partial(grads_kernel, j, n_hid, rows, first), in...  6.6 us
    pallas_call x1, Pallas kernels, fast_device(): pl.pallas_call(functools.partial(load_weights_kernel, share, places), in_...  5.58 us
    pallas_call x1, Pallas kernels, fast_device(): pl.pallas_call(functools.partial(adam_kernel, places, share), in_specs=[V...  1.45 us
  transfers between devices with their start and end apart: 25, of which 7 were waited for; matrix products, arithmetic and copies ran while one was open for 0% of the time, Pallas kernels for 29%

profile of v2, /device:TPU:0, one launch (start us, length us, event | category | flops | bytes accessed | tf_op | source)
XLA Modules:
  0.0 67.7 jit_solution(2446188341641980911)
XLA Ops:
  0.6 3.1 %collective-permute-start = (bf16[16,4096]{1,0:T(8,128)(2,1)}, bf16[16,4096]{1,0:T(8,128)(2,1)S(1)}, u32[]{:S(2)}, u32[]{:S(2)}) collective-permute-start(bf16[16,4096]{1,0:T(8,128)(2,1)} %refs_0_.2), channel_id=1, source_target_pairs={{0,1},{1,0},{2,3},{3,2},{4,5},{5,4},{6,7},{7,6},{8,9},{9,8},{10,11... | collective-permute-start | bytes 393224 | tf_op jit(solution)/shard_map/ppermute | solution.py:224
  3.7 2.6 %collective-permute-start.1 = (bf16[16,4096]{1,0:T(8,128)(2,1)}, bf16[16,4096]{1,0:T(8,128)(2,1)S(1)}, u32[]{:S(2)}, u32[]{:S(2)}) collective-permute-start(bf16[16,4096]{1,0:T(8,128)(2,1)} %refs_0_.2), channel_id=1, source_target_pairs={{0,2},{1,3},{2,0},{3,1},{4,6},{5,7},{6,4},{7,5},{8,10},{9,11},{10,... | collective-permute-start | bytes 393224 | tf_op jit(solution)/shard_map/ppermute | solution.py:224
  9.0 2.7 %collective-permute-start.10 = (bf16[512,256]{1,0:T(8,128)(2,1)}, bf16[512,256]{1,0:T(8,128)(2,1)S(1)}, u32[]{:S(2)}, u32[]{:S(2)}) collective-permute-start(bf16[512,256]{1,0:T(8,128)(2,1)} %basis.1), channel_id=1, source_target_pairs={{0,24},{4,28},{8,16},{12,20},{16,8},{20,12},{24,0},{28,4},{1,25},{... | collective-permute-start | bytes 786440 | tf_op jit(solution)/shard_map/ppermute | solution.py:224
  11.7 5.1 %collective-permute-done.1.refs_2_ = bf16[16,4096]{1,0:T(8,128)(2,1)S(1)} collective-permute-done((bf16[16,4096]{1,0:T(8,128)(2,1)}, bf16[16,4096]{1,0:T(8,128)(2,1)S(1)}, u32[]{:S(2)}, u32[]{:S(2)}) %collective-permute-start.1) | collective-permute-done | bytes 131104 | tf_op jit(solution)/shard_map/ppermute | solution.py:224
  16.8 1.5 %collective-permute-start.8 = (bf16[512,256]{1,0:T(8,128)(2,1)}, bf16[512,256]{1,0:T(8,128)(2,1)S(1)}, u32[]{:S(2)}, u32[]{:S(2)}) collective-permute-start(bf16[512,256]{1,0:T(8,128)(2,1)} %basis.1), channel_id=1, source_target_pairs={{0,8},{4,12},{8,0},{12,4},{16,24},{20,28},{24,16},{28,20},{1,9},{5... | collective-permute-start | bytes 786440 | tf_op jit(solution)/shard_map/ppermute | solution.py:224
  18.3 1.5 %collective-permute-start.9 = (bf16[512,256]{1,0:T(8,128)(2,1)}, bf16[512,256]{1,0:T(8,128)(2,1)S(1)}, u32[]{:S(2)}, u32[]{:S(2)}) collective-permute-start(bf16[512,256]{1,0:T(8,128)(2,1)} %basis.1), channel_id=1, source_target_pairs={{0,16},{4,20},{8,24},{12,28},{16,0},{20,4},{24,8},{28,12},{1,17},{... | collective-permute-start | bytes 786440 | tf_op jit(solution)/shard_map/ppermute | solution.py:224
  20.4 5.6 %load_weights.1.refs_8_.refs_1_ = bf16[4,2,240,4096]{3,2,1,0:T(8,128)(2,1)S(1)} custom-call(bf16[2,1920,4096]{2,1,0:T(8,128)(2,1)} %w_hbm.1), custom_call_target="tpu_custom_call" | custom-call | bytes 31457280 | tf_op jit(solution)/shard_map/load_weights/pallas_call | solution.py:250
  26.0 1.7 %shard_map.94 = (bf16[256,256]{1,0:T(8,128)(2,1)S(1)}, bf16[128,4096]{1,0:T(8,128)(2,1)S(1)}) custom-call(bf16[16,4096]{1,0:T(8,128)(2,1)S(1)} %copy-done.4, bf16[16,4096]{1,0:T(8,128)(2,1)S(1)} %collective-permute-done.refs_1_, bf16[16,4096]{1,0:T(8,128)(2,1)S(1)} %collective-permute-done.1.refs_2_, bf16[16,4096]{1,0:T(8,128)(2,1)S(1)} %collective-permute-done.2.refs_3_, ...), custom_call_target="tpu_custom_call" | custom-call | flops 503316480 | bytes 3932160 | tf_op jit(solution)/shard_map/pallas_call | solution.py:275
  28.2 1.7 %shard_map.97 = bf16[256,256]{1,0:T(8,128)(2,1)S(1)} custom-call(bf16[128,4096]{1,0:T(8,128)(2,1)S(1)} %get-tuple-element.20.refs_0_.tok, bf16[4,2,240,4096]{3,2,1,0:T(8,128)(2,1)S(1)} %load_weights.1.refs_8_.refs_1_, bf16[4,64,240]{2,1,0:T(8,128)(2,1)S(1)} %get-tuple-element.18.refs_9_.refs_2_, bf16[4,64,240]{2,1,0:T(8,128)(2,1)S(1)} %collective-permute-done.7.refs_10_.refs_3_), custom_call_target="tpu_custom_call" | custom-call | flops 503316480 | bytes 3932160 | tf_op jit(solution)/shard_map/pallas_call | solution.py:275
  30.5 1.7 %shard_map.96 = bf16[256,256]{1,0:T(8,128)(2,1)S(1)} custom-call(bf16[128,4096]{1,0:T(8,128)(2,1)S(1)} %get-tuple-element.20.refs_0_.tok, bf16[4,2,240,4096]{3,2,1,0:T(8,128)(2,1)S(1)} %load_weights.1.refs_8_.refs_1_, bf16[4,64,240]{2,1,0:T(8,128)(2,1)S(1)} %get-tuple-element.18.refs_9_.refs_2_, bf16[4,64,240]{2,1,0:T(8,128)(2,1)S(1)} %collective-permute-done.7.refs_10_.refs_3_), custom_call_target="tpu_custom_call" | custom-call | flops 503316480 | bytes 3932160 | tf_op jit(solution)/shard_map/pallas_call | solution.py:275
  32.9 2.4 %collective-permute-start.14 = (bf16[256,256]{1,0:T(8,128)(2,1)S(1)}, bf16[256,256]{1,0:T(8,128)(2,1)S(1)}, u32[]{:S(2)}, u32[]{:S(2)}) collective-permute-start(bf16[256,256]{1,0:T(8,128)(2,1)S(1)} %get-tuple-element.23), channel_id=1, source_target_pairs={{0,24},{4,28},{8,16},{12,20},{16,8},{20,12},{24,0},{28,4},{1,25},{... | collective-permute-start | bytes 393224 | tf_op jit(solution)/shard_map/ppermute | solution.py:224
  36.6 2.4 %collective-permute-start.17 = (bf16[144,256]{1,0:T(8,128)(2,1)S(1)}, bf16[144,256]{1,0:T(8,128)(2,1)S(1)}, u32[]{:S(2)}, u32[]{:S(2)}) collective-permute-start(bf16[144,256]{1,0:T(8,128)(2,1)S(1)} %get-tuple-element.24), channel_id=1, source_target_pairs={{0,24},{4,28},{8,16},{12,20},{16,8},{20,12},{24,0},{28,4},{1,25},{... | collective-permute-start | bytes 221192 | tf_op jit(solution)/shard_map/ppermute | solution.py:224
  39.4 1.5 %shard_map.95.own_grads = f32[2,128,240]{2,1,0:T(8,128)S(1)} custom-call(bf16[128,4096]{1,0:T(8,128)(2,1)S(1)} %get-tuple-element.20.refs_0_.tok, bf16[4,2,240,4096]{3,2,1,0:T(8,128)(2,1)S(1)} %load_weights.1.refs_8_.refs_1_, bf16[4,64,240]{2,1,0:T(8,128)(2,1)S(1)} %get-tuple-element.18.refs_9_.refs_2_, ...), custom_call_target="tpu_custom_call" | custom-call | flops 1000 | bytes 1000 | tf_op jit(solution)/shard_map/pallas_call | solution.py:275
  40.9 1.6 %collective-permute-done.14.refs_2_ = bf16[256,256]{1,0:T(8,128)(2,1)S(1)} collective-permute-done((bf16[256,256]{1,0:T(8,128)(2,1)S(1)}, bf16[256,256]{1,0:T(8,128)(2,1)S(1)}, u32[]{:S(2)}, u32[]{:S(2)}) %collective-permute-start.14) | collective-permute-done | bytes 131104 | tf_op jit(solution)/shard_map/ppermute | solution.py:224
  43.1 1.7 %collective-permute-done.17.refs_5_ = bf16[144,256]{1,0:T(8,128)(2,1)S(1)} collective-permute-done((bf16[144,256]{1,0:T(8,128)(2,1)S(1)}, bf16[144,256]{1,0:T(8,128)(2,1)S(1)}, u32[]{:S(2)}, u32[]{:S(2)}) %collective-permute-start.17) | collective-permute-done | bytes 73760 | tf_op jit(solution)/shard_map/ppermute | solution.py:224
  44.8 1.5 %adam.1 = (f32[2,240,256]{2,1,0:T(8,128)S(1)}, f32[2,240,256]{2,1,0:T(8,128)S(1)}, bf16[2,240,256]{2,1,0:T(8,128)(2,1)S(1)}) custom-call(f32[2,128,240]{2,1,0:T(8,128)S(1)} %shard_map.95.own_grads, f32[128,256]{1,0:T(8,128)S(1)} %get-tuple-element.21.part, f32[128,256]{1,0:T(8,128)S(1)} %collective-permute-done.11.part_other, ...), custom_call_target="tpu_custom_call" | custom-call | flops 1000 | bytes 1000 | tf_op jit(solution)/shard_map/adam/pallas_call | solution.py:331
  47.4 2.4 %collective-permute-start.20 = (bf16[2,240,256]{2,1,0:T(8,128)(2,1)S(1)}, bf16[2,240,256]{2,1,0:T(8,128)(2,1)S(1)}, u32[]{:S(2)}, u32[]{:S(2)}) collective-permute-start(bf16[2,240,256]{2,1,0:T(8,128)(2,1)S(1)} %get-tuple-element.27.refs_0_), channel_id=1, source_target_pairs={{0,24},{4,28},{8,16},{12,20},{16,8},{20,12},{24,0},{28,4},{1,25},{... | collective-permute-start | bytes 737288 | tf_op jit(solution)/shard_map/ppermute | solution.py:224
  49.8 5.3 %collective-permute-done.22.refs_0_ = bf16[2,240,256]{2,1,0:T(8,128)(2,1)S(1)} collective-permute-done((bf16[2,240,256]{2,1,0:T(8,128)(2,1)S(1)}, bf16[2,240,256]{2,1,0:T(8,128)(2,1)S(1)}, u32[]{:S(2)}, u32[]{:S(2)}) %collective-permute-start.22) | collective-permute-done | bytes 245792 | tf_op jit(solution)/shard_map/ppermute | solution.py:224
  55.2 3.6 %collective-permute-done.18.refs_0_ = bf16[2,240,256]{2,1,0:T(8,128)(2,1)S(1)} collective-permute-done((bf16[2,240,256]{2,1,0:T(8,128)(2,1)S(1)}, bf16[2,240,256]{2,1,0:T(8,128)(2,1)S(1)}, u32[]{:S(2)}, u32[]{:S(2)}) %collective-permute-start.18) | collective-permute-done | bytes 245792 | tf_op jit(solution)/shard_map/ppermute | solution.py:224
  59.3 1.2 %moments.1 = (f32[240,2,256]{2,1,0:T(2,128)}, f32[240,2,256]{2,1,0:T(2,128)}) custom-call(f32[2,240,256]{2,1,0:T(8,128)S(1)} %get-tuple-element.29.first, f32[2,240,256]{2,1,0:T(8,128)S(1)} %get-tuple-element.30.second), custom_call_target="tpu_custom_call" | custom-call | flops 1000 | bytes 1000 | tf_op jit(solution)/shard_map/moments/pallas_call | solution.py:351
  60.5 1.8 %shard_map.98.refs_4_ = f32[2,1920,512]{2,1,0:T(8,128)} custom-call(bf16[2,240,256]{2,1,0:T(8,128)(2,1)S(1)} %get-tuple-element.27.refs_0_, bf16[2,240,256]{2,1,0:T(8,128)(2,1)S(1)} %collective-permute-done.24.refs_1_, bf16[512,512]{1,0:T(8,128)(2,1)S(1)} %get-tuple-element.28.refs_2_, f32[2,1920,512]{2,1,0:T(8,128)S(1)} %bitcast.1), custom_call_target="tpu_custom_call" | custom-call | flops 503316480 | bytes 3932160 | tf_op jit(solution)/shard_map/pallas_call | solution.py:366
  62.3 1.8 %shard_map.99.refs_4_ = f32[2,1920,512]{2,1,0:T(8,128)} custom-call(bf16[2,240,256]{2,1,0:T(8,128)(2,1)S(1)} %collective-permute-done.22.refs_0_, bf16[2,240,256]{2,1,0:T(8,128)(2,1)S(1)} %collective-permute-done.23.refs_1_, bf16[512,512]{1,0:T(8,128)(2,1)S(1)} %get-tuple-element.28.refs_2_, ...), custom_call_target="tpu_custom_call", output_to_operand_aliasing={{}: (4, {})} | custom-call | flops 503316480 | bytes 3932160 | tf_op jit(solution)/shard_map/pallas_call | solution.py:366
  64.1 1.8 %shard_map.100.refs_4_ = f32[2,1920,512]{2,1,0:T(8,128)} custom-call(bf16[2,240,256]{2,1,0:T(8,128)(2,1)S(1)} %collective-permute-done.18.refs_0_, bf16[2,240,256]{2,1,0:T(8,128)(2,1)S(1)} %collective-permute-done.20.refs_1_, bf16[512,512]{1,0:T(8,128)(2,1)S(1)} %get-tuple-element.28.refs_2_, ...), custom_call_target="tpu_custom_call", output_to_operand_aliasing={{}: (4, {})} | custom-call | flops 503316480 | bytes 3932160 | tf_op jit(solution)/shard_map/pallas_call | solution.py:366
  65.9 1.8 %shard_map.101 = f32[2,1920,512]{2,1,0:T(8,128)} custom-call(bf16[2,240,256]{2,1,0:T(8,128)(2,1)S(1)} %collective-permute-done.19.refs_0_, bf16[2,240,256]{2,1,0:T(8,128)(2,1)S(1)} %collective-permute-done.21.refs_1_, bf16[512,512]{1,0:T(8,128)(2,1)S(1)} %get-tuple-element.28.refs_2_, f32[2,1920,512]{2,1,0:T(8,128)S(1)} %bitcast.1, ...), custom_call_target="tpu_custom_call", output_to_operand_aliasing={{}: (4, {})} | custom-call | flops 503316480 | bytes 3932160 | tf_op jit(solution)/shard_map/pallas_call | solution.py:366
  (56 shorter events, 8.8 us)
Async XLA Ops:
  0.6 8.4 %collective-permute-start = (bf16[16,4096]{1,0:T(8,128)(2,1)}, bf16[16,4096]{1,0:T(8,128)(2,1)S(1)}, u32[]{:S(2)}, u32[]{:S(2)}) collective-permute-start(bf16[16,4096]{1,0:T(8,128)(2,1)} %refs_0_.2), channel_id=1, source_target_pairs={{0,1},{1,0},{2,3},{3,2},{4,5},{5,4},{6,7},{7,6},{8,9},{9,8},{10,11... | collective-permute-start | bytes 393224 | tf_op jit(solution)/shard_map/ppermute | solution.py:224
  3.7 13.1 %collective-permute-start.1 = (bf16[16,4096]{1,0:T(8,128)(2,1)}, bf16[16,4096]{1,0:T(8,128)(2,1)S(1)}, u32[]{:S(2)}, u32[]{:S(2)}) collective-permute-start(bf16[16,4096]{1,0:T(8,128)(2,1)} %refs_0_.2), channel_id=1, source_target_pairs={{0,2},{1,3},{2,0},{3,1},{4,6},{5,7},{6,4},{7,5},{8,10},{9,11},{10,... | collective-permute-start | bytes 393224 | tf_op jit(solution)/shard_map/ppermute | solution.py:224
  6.3 12.0 %collective-permute-start.2 = (bf16[16,4096]{1,0:T(8,128)(2,1)}, bf16[16,4096]{1,0:T(8,128)(2,1)S(1)}, u32[]{:S(2)}, u32[]{:S(2)}) collective-permute-start(bf16[16,4096]{1,0:T(8,128)(2,1)} %refs_0_.2), channel_id=1, source_target_pairs={{0,3},{1,2},{2,1},{3,0},{4,7},{5,6},{6,5},{7,4},{8,11},{9,10},{10,... | collective-permute-start | bytes 393224 | tf_op jit(solution)/shard_map/ppermute | solution.py:224
  7.6 12.3 %collective-permute-start.3 = (bf16[16,4096]{1,0:T(8,128)(2,1)}, bf16[16,4096]{1,0:T(8,128)(2,1)S(1)}, u32[]{:S(2)}, u32[]{:S(2)}) collective-permute-start(bf16[16,4096]{1,0:T(8,128)(2,1)} %refs_0_.2), channel_id=1, source_target_pairs={{0,4},{4,0},{8,12},{12,8},{16,20},{20,16},{24,28},{28,24},{1,5},{5... | collective-permute-start | bytes 393224 | tf_op jit(solution)/shard_map/ppermute | solution.py:224
  9.0 10.8 %collective-permute-start.4 = (bf16[16,4096]{1,0:T(8,128)(2,1)S(1)}, bf16[16,4096]{1,0:T(8,128)(2,1)S(1)}, u32[]{:S(2)}, u32[]{:S(2)}) collective-permute-start(bf16[16,4096]{1,0:T(8,128)(2,1)S(1)} %collective-permute-done.refs_1_), channel_id=1, source_target_pairs={{0,4},{4,0},{8,12},{12,8},{16,20},{20,16},{24,28},{28,24},{1,5},{5... | collective-permute-start | bytes 393224 | tf_op jit(solution)/shard_map/ppermute | solution.py:224
  9.0 18.7 %collective-permute-start.10 = (bf16[512,256]{1,0:T(8,128)(2,1)}, bf16[512,256]{1,0:T(8,128)(2,1)S(1)}, u32[]{:S(2)}, u32[]{:S(2)}) collective-permute-start(bf16[512,256]{1,0:T(8,128)(2,1)} %basis.1), channel_id=1, source_target_pairs={{0,24},{4,28},{8,16},{12,20},{16,8},{20,12},{24,0},{28,4},{1,25},{... | collective-permute-start | bytes 786440 | tf_op jit(solution)/shard_map/ppermute | solution.py:224
  16.8 10.9 %collective-permute-start.8 = (bf16[512,256]{1,0:T(8,128)(2,1)}, bf16[512,256]{1,0:T(8,128)(2,1)S(1)}, u32[]{:S(2)}, u32[]{:S(2)}) collective-permute-start(bf16[512,256]{1,0:T(8,128)(2,1)} %basis.1), channel_id=1, source_target_pairs={{0,8},{4,12},{8,0},{12,4},{16,24},{20,28},{24,16},{28,20},{1,9},{5... | collective-permute-start | bytes 786440 | tf_op jit(solution)/shard_map/ppermute | solution.py:224
  18.3 9.4 %collective-permute-start.9 = (bf16[512,256]{1,0:T(8,128)(2,1)}, bf16[512,256]{1,0:T(8,128)(2,1)S(1)}, u32[]{:S(2)}, u32[]{:S(2)}) collective-permute-start(bf16[512,256]{1,0:T(8,128)(2,1)} %basis.1), channel_id=1, source_target_pairs={{0,16},{4,20},{8,24},{12,28},{16,0},{20,4},{24,8},{28,12},{1,17},{... | collective-permute-start | bytes 786440 | tf_op jit(solution)/shard_map/ppermute | solution.py:224
  19.9 6.1 %collective-permute-start.5 = (bf16[16,4096]{1,0:T(8,128)(2,1)S(1)}, bf16[16,4096]{1,0:T(8,128)(2,1)S(1)}, u32[]{:S(2)}, u32[]{:S(2)}) collective-permute-start(bf16[16,4096]{1,0:T(8,128)(2,1)S(1)} %collective-permute-done.1.refs_2_), channel_id=1, source_target_pairs={{0,4},{4,0},{8,12},{12,8},{16,20},{20,16},{24,28},{28,24},{1,5},{5... | collective-permute-start | bytes 393224 | tf_op jit(solution)/shard_map/ppermute | solution.py:224
  19.9 6.1 %collective-permute-start.6 = (bf16[16,4096]{1,0:T(8,128)(2,1)S(1)}, bf16[16,4096]{1,0:T(8,128)(2,1)S(1)}, u32[]{:S(2)}, u32[]{:S(2)}) collective-permute-start(bf16[16,4096]{1,0:T(8,128)(2,1)S(1)} %collective-permute-done.2.refs_3_), channel_id=1, source_target_pairs={{0,4},{4,0},{8,12},{12,8},{16,20},{20,16},{24,28},{28,24},{1,5},{5... | collective-permute-start | bytes 393224 | tf_op jit(solution)/shard_map/ppermute | solution.py:224
  28.1 7.2 %collective-permute-start.11 = (f32[128,256]{1,0:T(8,128)S(1)}, f32[128,256]{1,0:T(8,128)S(1)}, u32[]{:S(2)}, u32[]{:S(2)}) collective-permute-start(f32[128,256]{1,0:T(8,128)S(1)} %get-tuple-element.22), channel_id=1, source_target_pairs={{0,4},{4,0},{8,12},{12,8},{16,20},{20,16},{24,28},{28,24},{1,5},{5... | collective-permute-start | bytes 393224 | tf_op jit(solution)/shard_map/ppermute | solution.py:224
  30.0 6.7 %collective-permute-start.13 = (bf16[256,256]{1,0:T(8,128)(2,1)S(1)}, bf16[256,256]{1,0:T(8,128)(2,1)S(1)}, u32[]{:S(2)}, u32[]{:S(2)}) collective-permute-start(bf16[256,256]{1,0:T(8,128)(2,1)S(1)} %shard_map.97), channel_id=1, source_target_pairs={{0,16},{4,20},{8,24},{12,28},{16,0},{20,4},{24,8},{28,12},{1,17},{... | collective-permute-start | bytes 393224 | tf_op jit(solution)/shard_map/ppermute | solution.py:224
  32.3 8.6 %collective-permute-start.12 = (bf16[256,256]{1,0:T(8,128)(2,1)S(1)}, bf16[256,256]{1,0:T(8,128)(2,1)S(1)}, u32[]{:S(2)}, u32[]{:S(2)}) collective-permute-start(bf16[256,256]{1,0:T(8,128)(2,1)S(1)} %shard_map.96), channel_id=1, source_target_pairs={{0,8},{4,12},{8,0},{12,4},{16,24},{20,28},{24,16},{28,20},{1,9},{5... | collective-permute-start | bytes 393224 | tf_op jit(solution)/shard_map/ppermute | solution.py:224
  32.9 9.6 %collective-permute-start.14 = (bf16[256,256]{1,0:T(8,128)(2,1)S(1)}, bf16[256,256]{1,0:T(8,128)(2,1)S(1)}, u32[]{:S(2)}, u32[]{:S(2)}) collective-permute-start(bf16[256,256]{1,0:T(8,128)(2,1)S(1)} %get-tuple-element.23), channel_id=1, source_target_pairs={{0,24},{4,28},{8,16},{12,20},{16,8},{20,12},{24,0},{28,4},{1,25},{... | collective-permute-start | bytes 393224 | tf_op jit(solution)/shard_map/ppermute | solution.py:224
  35.5 7.5 %collective-permute-start.15 = (bf16[144,256]{1,0:T(8,128)(2,1)S(1)}, bf16[144,256]{1,0:T(8,128)(2,1)S(1)}, u32[]{:S(2)}, u32[]{:S(2)}) collective-permute-start(bf16[144,256]{1,0:T(8,128)(2,1)S(1)} %get-tuple-element.24), channel_id=1, source_target_pairs={{0,8},{4,12},{8,0},{12,4},{16,24},{20,28},{24,16},{28,20},{1,9},{5... | collective-permute-start | bytes 221192 | tf_op jit(solution)/shard_map/ppermute | solution.py:224
  36.1 6.9 %collective-permute-start.16 = (bf16[144,256]{1,0:T(8,128)(2,1)S(1)}, bf16[144,256]{1,0:T(8,128)(2,1)S(1)}, u32[]{:S(2)}, u32[]{:S(2)}) collective-permute-start(bf16[144,256]{1,0:T(8,128)(2,1)S(1)} %get-tuple-element.24), channel_id=1, source_target_pairs={{0,16},{4,20},{8,24},{12,28},{16,0},{20,4},{24,8},{28,12},{1,17},{... | collective-permute-start | bytes 221192 | tf_op jit(solution)/shard_map/ppermute | solution.py:224
  36.6 8.2 %collective-permute-start.17 = (bf16[144,256]{1,0:T(8,128)(2,1)S(1)}, bf16[144,256]{1,0:T(8,128)(2,1)S(1)}, u32[]{:S(2)}, u32[]{:S(2)}) collective-permute-start(bf16[144,256]{1,0:T(8,128)(2,1)S(1)} %get-tuple-element.24), channel_id=1, source_target_pairs={{0,24},{4,28},{8,16},{12,20},{16,8},{20,12},{24,0},{28,4},{1,25},{... | collective-permute-start | bytes 221192 | tf_op jit(solution)/shard_map/ppermute | solution.py:224
  46.3 8.9 %collective-permute-start.22 = (bf16[2,240,256]{2,1,0:T(8,128)(2,1)S(1)}, bf16[2,240,256]{2,1,0:T(8,128)(2,1)S(1)}, u32[]{:S(2)}, u32[]{:S(2)}) collective-permute-start(bf16[2,240,256]{2,1,0:T(8,128)(2,1)S(1)} %get-tuple-element.27.refs_0_), channel_id=1, source_target_pairs={{0,8},{4,12},{8,0},{12,4},{16,24},{20,28},{24,16},{28,20},{1,9},{5... | collective-permute-start | bytes 737288 | tf_op jit(solution)/shard_map/ppermute | solution.py:224
  46.9 11.8 %collective-permute-start.18 = (bf16[2,240,256]{2,1,0:T(8,128)(2,1)S(1)}, bf16[2,240,256]{2,1,0:T(8,128)(2,1)S(1)}, u32[]{:S(2)}, u32[]{:S(2)}) collective-permute-start(bf16[2,240,256]{2,1,0:T(8,128)(2,1)S(1)} %get-tuple-element.27.refs_0_), channel_id=1, source_target_pairs={{0,16},{4,20},{8,24},{12,28},{16,0},{20,4},{24,8},{28,12},{1,17},{... | collective-permute-start | bytes 737288 | tf_op jit(solution)/shard_map/ppermute | solution.py:224
  47.4 11.4 %collective-permute-start.20 = (bf16[2,240,256]{2,1,0:T(8,128)(2,1)S(1)}, bf16[2,240,256]{2,1,0:T(8,128)(2,1)S(1)}, u32[]{:S(2)}, u32[]{:S(2)}) collective-permute-start(bf16[2,240,256]{2,1,0:T(8,128)(2,1)S(1)} %get-tuple-element.27.refs_0_), channel_id=1, source_target_pairs={{0,24},{4,28},{8,16},{12,20},{16,8},{20,12},{24,0},{28,4},{1,25},{... | collective-permute-start | bytes 737288 | tf_op jit(solution)/shard_map/ppermute | solution.py:224
  49.8 10.6 %collective-permute-start.24 = (bf16[2,240,256]{2,1,0:T(8,128)(2,1)S(1)}, bf16[2,240,256]{2,1,0:T(8,128)(2,1)S(1)}, u32[]{:S(2)}, u32[]{:S(2)}) collective-permute-start(bf16[2,240,256]{2,1,0:T(8,128)(2,1)S(1)} %get-tuple-element.27.refs_0_), channel_id=1, source_target_pairs={{0,4},{4,0},{8,12},{12,8},{16,20},{20,16},{24,28},{28,24},{1,5},{5... | collective-permute-start | bytes 737288 | tf_op jit(solution)/shard_map/ppermute | solution.py:224
  55.2 7.1 %collective-permute-start.23 = (bf16[2,240,256]{2,1,0:T(8,128)(2,1)S(1)}, bf16[2,240,256]{2,1,0:T(8,128)(2,1)S(1)}, u32[]{:S(2)}, u32[]{:S(2)}) collective-permute-start(bf16[2,240,256]{2,1,0:T(8,128)(2,1)S(1)} %collective-permute-done.22.refs_0_), channel_id=1, source_target_pairs={{0,4},{4,0},{8,12},{12,8},{16,20},{20,16},{24,28},{28,24},{1,5},{5... | collective-permute-start | bytes 737288 | tf_op jit(solution)/shard_map/ppermute | solution.py:224
  58.8 7.1 %collective-permute-start.19 = (bf16[2,240,256]{2,1,0:T(8,128)(2,1)S(1)}, bf16[2,240,256]{2,1,0:T(8,128)(2,1)S(1)}, u32[]{:S(2)}, u32[]{:S(2)}) collective-permute-start(bf16[2,240,256]{2,1,0:T(8,128)(2,1)S(1)} %collective-permute-done.18.refs_0_), channel_id=1, source_target_pairs={{0,4},{4,0},{8,12},{12,8},{16,20},{20,16},{24,28},{28,24},{1,5},{5... | collective-permute-start | bytes 737288 | tf_op jit(solution)/shard_map/ppermute | solution.py:224
  58.8 7.1 %collective-permute-start.21 = (bf16[2,240,256]{2,1,0:T(8,128)(2,1)S(1)}, bf16[2,240,256]{2,1,0:T(8,128)(2,1)S(1)}, u32[]{:S(2)}, u32[]{:S(2)}) collective-permute-start(bf16[2,240,256]{2,1,0:T(8,128)(2,1)S(1)} %collective-permute-done.20.refs_1_), channel_id=1, source_target_pairs={{0,4},{4,0},{8,12},{12,8},{16,20},{20,16},{24,28},{28,24},{1,5},{5... | collective-permute-start | bytes 737288 | tf_op jit(solution)/shard_map/ppermute | solution.py:224
  (8 other events, 83.5 us)
